TPU v7x, 32 devices: a whole 2x2x4 slice. The times are simulated.
32 devices in a mesh: groups: 2 (over x), freq: 16 (over z, y, core).
Axes of the slice: x: 2, y: 2, z: 4, core: 2. Of those that a mesh axis runs over, the one named last changes fastest.
Arguments:
- voltages: bfloat16 [32, 263, 2, 2, 2048], P(('groups', 'freq')), parts along dimension 0, may hold values from -12 to 12
- pfb_taps: float32 [8, 2], replicated, may hold values from 0.2 to 1
- steering: bfloat16 [64, 2, 2048, 64], P(('groups', 'freq')), parts along dimension 0, may hold values from -0.09375 to 0.09375
- fdmt_offsets: int32 [5, 2, 128], replicated, may hold values from 0 to 63, as said below
- box_lengths: int32 [8], replicated, may hold values from 1 to 64, as said below
Outputs:
- dedispersed: float32 [256, 64, 256], P(('groups', 'freq')), parts along dimension 0
- box_scores: float32 [256, 8, 64], P(('groups', 'freq')), parts along dimension 0
- peak_per_beam: float32 [128], P('groups'), parts along dimension 0
There are 2 independent parts, one for each index of `groups`. A program takes and returns all parts, laid end to end along the dimension named above; an argument that names none is the same for every part. Nothing has to cross between parts.
Inputs may be any that keep to these rules, and one draw needn't show every extreme that they name: `fdmt_offsets`: at level k every entry is below 4 * 2^k. Within each merged subband both rows are nondecreasing in d and rise by at most one per step; their sum is d except where the upper row stops at its largest value. `box_lengths`: the last filter is exactly 64 samples long.
All inputs are finite; a program needn't handle non-finite values.
Results may differ from a plain program's by a relative error of at most 0.0024.
The roundings to bfloat16 on the way count: a program that leaves them out, or rounds other values in their place, can miss the bound.
Values sent between devices are 32-bit elements; how exact they have to be, the bound alone decides.
No kernel may reach another device: no remote copies, remote signals or barrier semaphores. Data moves between devices by JAX's collectives and lax.ppermute only.
A program may use at most 64 MiB of HBM per device.

v0:
```python
import math

import jax
import jax.numpy as jnp
from jax import lax
from jax.sharding import PartitionSpec as P


def shift_time(value_array, amount):
    length = value_array.shape[-1]
    if amount >= length:
        return jnp.zeros_like(value_array)
    zeros_part = jnp.zeros(value_array.shape[:-1] + (amount,), value_array.dtype)
    return jnp.concatenate([zeros_part, value_array[..., : length - amount]], axis=-1)


def delay_rows(value_array, lag_rows, child_rows):
    result = value_array
    for section_bit in range(max(child_rows - 1, 0).bit_length()):
        step_size = 1 << section_bit
        chosen = lag_rows >> section_bit & 1 == 1
        result = jnp.where(chosen[:, :, None, None], shift_time(result, step_size), result)
    return result


def take_band(band_rows, row_index):
    return jnp.take(band_rows, row_index, axis=0)


def merge_bands(lower_band, upper_band, low_rows, high_rows):
    child_rows = lower_band.shape[1]
    from_lower = jax.vmap(take_band)(lower_band, low_rows)
    from_upper = delay_rows(jax.vmap(take_band)(upper_band, high_rows), low_rows, child_rows)
    return from_lower + from_upper


def first_plane(cleaned, delay_rate):
    running_sum = cleaned
    term_list = [cleaned]
    for lag_count in range(1, delay_rate):
        running_sum = running_sum + shift_time(cleaned, lag_count)
        term_list.append(running_sum)
    return jnp.stack(term_list, 1)


def normalize(power_rows):
    level_mean = jnp.mean(power_rows, axis=-1, keepdims=True)
    centered = power_rows - level_mean
    spread = jnp.mean(centered * centered, axis=-1, keepdims=True)
    return centered / jnp.sqrt(spread + 1e-05)


def beam_powers(volume, pfb_taps, weight_pair):
    tap_total = pfb_taps.shape[0]
    samples = volume.shape[0] - tap_total + 1
    beam_total = weight_pair.shape[-1]
    filtered = pfb_taps[0][None, :, None, None] * volume[0:samples].astype(jnp.float32)
    for tap_index in range(1, tap_total):
        filtered = filtered + pfb_taps[tap_index][None, :, None, None] * volume[
            tap_index : tap_index + samples
        ].astype(jnp.float32)
    fine_sum = (filtered[:, 0] + filtered[:, 1]).astype(jnp.bfloat16)
    fine_diff = (filtered[:, 0] - filtered[:, 1]).astype(jnp.bfloat16)
    powers = []
    for channel, fine_data in enumerate((fine_sum, fine_diff)):
        weights = weight_pair[channel]
        stacked = jnp.concatenate(
            [
                jnp.concatenate([weights[0], weights[1]], 1),
                jnp.concatenate([-weights[1], weights[0]], 1),
            ],
            0,
        )
        beam_out = jnp.einsum(
            "kb,sk->bs", stacked, fine_data.reshape(samples, -1), preferred_element_type=jnp.float32
        )
        real_part = beam_out[:beam_total]
        imag_part = beam_out[beam_total:]
        powers.append(real_part * real_part + imag_part * imag_part)
    return jnp.stack(powers, 1)


def shards(voltages, pfb_taps, steering, fdmt_offsets, box_lengths):
    devices = lax.axis_size("freq")
    device_id = lax.axis_index("freq")
    beam_total = steering.shape[-1]
    level_count = fdmt_offsets.shape[0]
    delays = fdmt_offsets.shape[-1]
    channels = 2 * devices
    delay_rate = delays // channels
    top_bit = devices.bit_length() - 2
    per_device = 2 * beam_total // devices
    half_rows = delays // 2
    half_index = device_id >> top_bit
    final_rows = lax.dynamic_slice_in_dim(
        fdmt_offsets[level_count - 1], half_index * half_rows, half_rows, axis=1
    )
    normed = normalize(beam_powers(voltages[0], pfb_taps, steering))
    outgoing = jnp.broadcast_to(normed[None], (2,) + normed.shape).reshape(
        devices, per_device, 2, normed.shape[-1]
    )
    incoming = lax.all_to_all(outgoing, "freq", split_axis=0, concat_axis=0, tiled=True)
    by_channel = jnp.transpose(incoming, (0, 2, 1, 3)).reshape(channels, per_device, -1)
    cleaned = by_channel - jnp.mean(by_channel, axis=0, keepdims=True)
    plane_now = first_plane(cleaned, delay_rate)
    for level_index in range(level_count - 1):
        band_count = plane_now.shape[0]
        child_rows = plane_now.shape[1]
        paired = plane_now.reshape(band_count // 2, 2, child_rows, per_device, plane_now.shape[-1])
        level_rows = fdmt_offsets[level_index].reshape(2, band_count // 2, 2 * child_rows)
        plane_now = merge_bands(paired[:, 0], paired[:, 1], level_rows[0], level_rows[1])
    final_plane = merge_bands(plane_now[0:1], plane_now[1:2], final_rows[0:1], final_rows[1:2])[0]
    scaled = final_plane / math.sqrt(channels)
    dedispersed = jnp.transpose(scaled, (1, 0, 2))
    samples = dedispersed.shape[-1]
    running = jnp.cumsum(dedispersed, axis=-1)
    padded = jnp.concatenate([jnp.zeros(running.shape[:-1] + (samples,), jnp.float32), running], -1)
    score_list = []
    for box_index in range(box_lengths.shape[0]):
        box_width = box_lengths[box_index]
        lagged = lax.dynamic_slice_in_dim(padded, samples - box_width, samples, axis=2)
        score_list.append(
            jnp.max((running - lagged) / jnp.sqrt(box_width.astype(jnp.float32)), axis=-1)
        )
    box_scores = jnp.stack(score_list, 1)
    local_best = jnp.max(box_scores, axis=(1, 2))
    beam_start = device_id % (devices // 2) * per_device
    contrib = lax.dynamic_update_slice(
        jnp.full((beam_total,), -1e30, jnp.float32), local_best, (beam_start,)
    )
    peak_per_beam = lax.pmax(contrib, "freq")
    return (dedispersed, box_scores, peak_per_beam)


def solution(mesh):
    placed = (
        P(("groups", "freq"), None, None, None, None),
        P(),
        P(("groups", "freq"), None, None, None),
        P(),
        P(),
    )
    return jax.shard_map(
        shards,
        mesh=mesh,
        in_specs=placed,
        out_specs=(
            P(("groups", "freq"), None, None),
            P(("groups", "freq"), None, None),
            P("groups"),
        ),
        check_vma=False,
    )
```

profile of v0, /device:TPU:0, one launch (start us, length us, event | category | flops | bytes accessed | tf_op | source)
XLA Modules:
  0.0 134.0 jit_solution(6319524763034091593)
XLA Ops:
  0.6 1.3 slice_bitcast_fusion.10
  1.9 1.1 fusion.53
  3.0 1.3 slice_reduce_fusion.7
  4.2 28.8 %fusion = f32[256,2,2,2048]{3,2,1,0:T(2,128)S(1)} fusion(f32[2]{0:T(128)S(1)} %get-tuple-element.47, f32[2]{0:T(128)S(1)} %get-tuple-element.48, f32[2]{0:T(128)S(1)} %get-tuple-element.42, f32[2]{0:T(128)S(1)} %get-tuple-element.43, f32[2]{0:T(128)S(1)} %get-tuple-element.44, f32[2]{0:T(128)S(1)} %get-tuple-element.45, f32[2]{0:T(128)S(1)} %get-tuple-element.46, ...), kind=kLoop, calls=%fused_computation.11 | loop fusion | flops 48234496 | bytes 41943104 | tf_op jit(solution)/shard_map/add | solution.py:59
  33.1 3.9 %add_convert_fusion = (bf16[256,1,2,2048]{3,2,1,0:T(2,128)(2,1)S(1)}, bf16[256,1,2,2048]{3,2,1,0:T(2,128)(2,1)S(1)}) fusion(f32[256,2,2,2048]{3,2,1,0:T(2,128)S(1)} %fusion), kind=kLoop, calls=%fused_computation.26 | loop fusion | flops 4194304 | bytes 12582912 | tf_op jit(solution)/shard_map/convert_element_type | solution.py:62
  36.9 0.9 copy.48
  37.8 0.9 copy.49
  38.8 0.8 fusion.7
  39.6 0.8 fusion.15
  40.9 0.7 copy.37
  41.7 7.4 %all-to-all-start = ((f32[16,8,2,256]{3,1,2,0:T(8,128)}), f32[16,8,2,256]{3,1,2,0:T(8,128)S(1)}, u32[]{:S(2)}, u32[]{:S(2)}) async-start(f32[16,8,2,256]{3,1,2,0:T(8,128)} %copy.37), calls=%async_computation | async-start | bytes 524288 | tf_op jit(solution)/shard_map/all_to_all | solution.py:102
  50.3 0.7 fusion.64
  67.3 0.3 pad_add_fusion
  67.8 1.0 gather_fusion.1
  69.1 0.6 pad_select_fusion.9
  69.7 1.0 gather_fusion
  70.7 0.7 select_add_fusion.3
  71.6 1.0 gather_fusion.3
  72.9 0.6 pad_select_fusion.8
  73.5 0.5 pad_select_fusion.7
  74.0 1.0 gather_fusion.2
  75.0 0.8 select_add_fusion.2
  75.9 1.0 gather_fusion.5
  77.1 0.6 pad_select_fusion.6
  77.8 0.5 pad_select_fusion.5
  78.3 0.5 pad_select_fusion.4
  78.8 1.0 gather_fusion.4
  79.8 1.0 select_add_fusion.1
  80.9 1.0 gather_fusion.7
  82.1 0.6 pad_select_fusion.3
  82.8 0.5 pad_select_fusion.2
  83.3 0.5 pad_select_fusion.1
  83.7 0.5 pad_select_fusion
  84.2 1.0 gather_fusion.6
  85.3 0.8 select_add_fusion
  86.1 0.7 gather_fusion.9
  86.9 0.3 pad_select_fusion.14
  87.3 0.3 pad_select_fusion.13
  87.5 0.3 pad_select_fusion.12
  87.8 0.3 pad_select_fusion.11
  88.4 0.7 gather_fusion.8
  89.0 0.3 fusion.40
  89.5 4.8 %reduce-window.6 = f32[8,64,2,128]{3,1,2,0:T(8,128)S(1)} reduce-window(f32[8,64,2,128]{3,1,2,0:T(8,128)S(1)} %copy.42, f32[]{:T(128)} %constant.60.clone.1), window={size=1x1x1x128 pad=0_0x0_0x0_0x127_0}, to_apply=%region_3.9 | reduce-window | flops 16646144 | bytes 1048580 | tf_op jit(solution)/shard_map/reduce-window
  95.0 1.0 fusion.38
  97.2 0.4 fusion.26
  98.1 34.3 %pmax.7 = f32[64]{0:T(128)} all-reduce(f32[64]{0:T(128)S(1)} %maximum_dynamic-update-slice_fusion), channel_id=1, replica_groups=mesh['groups'=2,'freq'=16] {'freq'}, use_global_device_ids=true, to_apply=%region_21.27 | all-reduce | flops 64 | bytes 512 | tf_op jit(solution)/shard_map/pmax | solution.py:131
  132.4 1.0 copy.46
  133.3 0.7 stack.64
  (86 shorter events, 6.5 us)
Async XLA Ops:
  39.6 9.5 %copy-start.1 = (s32[5,2,128]{2,1,0:T(2,128)S(1)}, s32[5,2,128]{2,1,0:T(2,128)}, u32[]{:S(2)}) copy-start(s32[5,2,128]{2,1,0:T(2,128)} %param.18) | copy-start | bytes 15364
  39.6 10.0 %slice-start = ((s32[5,2,128]{2,1,0:T(2,128)}), s32[1,2,128]{2,1,0:T(2,128)S(1)}, s32[]{:S(2)}) async-start(s32[5,2,128]{2,1,0:T(2,128)} %param.18), calls=%async_computation.1 | async-start | bytes 2048 | tf_op jit(solution)/shard_map/slice | solution.py:96
  39.6 10.6 %copy-start = (s32[8]{0:T(128)S(1)}, s32[8]{0:T(128)}, u32[]{:S(2)}) copy-start(s32[8]{0:T(128)} %param.19) | copy-start | bytes 100
  41.7 25.5 %all-to-all-start = ((f32[16,8,2,256]{3,1,2,0:T(8,128)}), f32[16,8,2,256]{3,1,2,0:T(8,128)S(1)}, u32[]{:S(2)}, u32[]{:S(2)}) async-start(f32[16,8,2,256]{3,1,2,0:T(8,128)} %copy.37), calls=%async_computation | async-start | bytes 524288 | tf_op jit(solution)/shard_map/all_to_all | solution.py:102
where the time goes:
time: 134 us
  other arithmetic  54.1 us (40%)
  blocking collectives  34.3 us (26%)
  local copies, waits for them, and re-layouts  19.7 us (15%)
  between operations  16.8 us (13%)
  starting transfers between devices  7.42 us (6%)
  matrix products  1.67 us (1%)
    pmax x1, blocking collectives, shards(): peak_per_beam = lax.pmax(contrib, 'freq')  34.3 us
    add x1, other arithmetic, beam_powers(): filtered + pfb_taps[tap_index][None, :, None, None] * volume[tap_index:ta...  28.8 us
    gather x23, local copies, waits for them, and re-layouts, take_band(): return jnp.take(band_rows, row_index, axis=0)  10.6 us
    all_to_all x1, starting transfers between devices, shards(): lax.all_to_all(outgoing, 'freq', split_axis=0, concat_axis=0, tiled=True)  7.42 us
    select_n x15, other arithmetic, delay_rows(): jnp.where(chosen[:, :, None, None], shift_time(result, step_size), result)  6.81 us
    another operation x3, other arithmetic  5.04 us
    convert_element_type x1, other arithmetic, beam_powers(): fine_sum = (filtered[:, 0] + filtered[:, 1]).astype(jnp.bfloat16)  3.85 us
    add x4, other arithmetic, merge_bands(): return from_lower + from_upper  3.21 us
  transfers between devices with their start and end apart: 1, of which 0 were waited for; matrix products, arithmetic and copies ran while one was open for 2% of the time, Pallas kernels for 0%

commit v1 on v0

--- a/solution.py
+++ b/solution.py
@@ -128,7 +128,12 @@
     contrib = lax.dynamic_update_slice(
         jnp.full((beam_total,), -1e30, jnp.float32), local_best, (beam_start,)
     )
-    peak_per_beam = lax.pmax(contrib, "freq")
+    peak_per_beam = contrib
+    step = 1
+    while step < devices:
+        pairs = [(place, place ^ step) for place in range(devices)]
+        peak_per_beam = jnp.maximum(peak_per_beam, lax.ppermute(peak_per_beam, "freq", pairs))
+        step *= 2
     return (dedispersed, box_scores, peak_per_beam)
 
 

time: 134 us -> 112 us (0.84)
  blocking collectives: 34.3 us -> 0 us
  starting transfers between devices: 7.42 us -> 14.3 us
  waiting for transfers between devices: 0.01 us -> 4.33 us
    pmax x1 -> x0, blocking collectives: 34.3 us -> none  [shards(): peak_per_beam = lax.pmax(contrib, 'freq')]
    ppermute x0 -> x4, starting transfers between devices: none -> 6.88 us  [shards(): lax.ppermute(peak_per_beam, 'freq', pairs)]
    ppermute x0 -> x4, waiting for transfers between devices: none -> 4.32 us  [shards(): lax.ppermute(peak_per_beam, 'freq', pairs)]
  transfers between devices with their start and end apart: 1 -> 5, of which waited for: 0 -> 4; matrix products, arithmetic and copies ran while one was open for 2% -> 4% of each run, Pallas kernels for 0% -> 0%
where the time goes in v1:
time: 112 us; the launch traced here: 111 us
  other arithmetic  54.6 us (49%)
  local copies, waits for them, and re-layouts  19.7 us (18%)
  between operations  16.8 us (15%)
  starting transfers between devices  14.3 us (13%)
  waiting for transfers between devices  4.33 us (4%)
  matrix products  1.67 us (1%)
    add x1, other arithmetic, beam_powers(): filtered + pfb_taps[tap_index][None, :, None, None] * volume[tap_index:ta...  28.8 us
    gather x23, local copies, waits for them, and re-layouts, take_band(): return jnp.take(band_rows, row_index, axis=0)  10.6 us
    all_to_all x1, starting transfers between devices, shards(): lax.all_to_all(outgoing, 'freq', split_axis=0, concat_axis=0, tiled=True)  7.42 us
    ppermute x4, starting transfers between devices, shards(): lax.ppermute(peak_per_beam, 'freq', pairs)  6.88 us
    select_n x15, other arithmetic, delay_rows(): jnp.where(chosen[:, :, None, None], shift_time(result, step_size), result)  6.81 us
    another operation x3, other arithmetic  5.04 us
    ppermute x4, waiting for transfers between devices, shards(): lax.ppermute(peak_per_beam, 'freq', pairs)  4.32 us
    convert_element_type x1, other arithmetic, beam_powers(): fine_sum = (filtered[:, 0] + filtered[:, 1]).astype(jnp.bfloat16)  3.85 us
  transfers between devices with their start and end apart: 5, of which 4 were waited for; matrix products, arithmetic and copies ran while one was open for 4% of the time, Pallas kernels for 0%

profile of v1, /device:TPU:0, one launch (start us, length us, event | category | flops | bytes accessed | tf_op | source)
XLA Modules:
  0.0 111.4 jit_solution(1818562661228296800)
XLA Ops:
  0.6 1.3 %slice_bitcast_fusion.10 = (bf16[2048,64]{0,1:T(8,128)(2,1)S(1)}, bf16[2048,64]{0,1:T(8,128)(2,1)S(1)}, bf16[2048,64]{0,1:T(8,128)(2,1)S(1)}, bf16[2048,64]{0,1:T(8,128)(2,1)S(1)}) fusion(bf16[2,2,2048,64]{2,3,1,0:T(8,128)(2,1)} %param.17), kind=kLoop, calls=%fused_computation.114 | loop fusion | bytes 2097152 | tf_op jit(solution)/shard_map/squeeze | solution.py:69
  1.9 1.1 fusion.53
  3.0 1.3 %slice_reduce_fusion.7 = (f32[2]{0:T(128)S(1)}, f32[2]{0:T(128)S(1)}, f32[2]{0:T(128)S(1)}, f32[2]{0:T(128)S(1)}, f32[2]{0:T(128)S(1)}, /*index=5*/f32[2]{0:T(128)S(1)}, f32[2]{0:T(128)S(1)}, f32[2]{0:T(128)S(1)}) fusion(f32[8,2]{0,1:T(2,128)} %param.16), kind=kLoop, calls=%fused_computation.196 | loop fusion | bytes 128 | tf_op jit(solution)/shard_map/slice | solution.py:57
  4.2 28.8 %fusion = f32[256,2,2,2048]{3,2,1,0:T(2,128)S(1)} fusion(f32[2]{0:T(128)S(1)} %get-tuple-element.47, f32[2]{0:T(128)S(1)} %get-tuple-element.48, f32[2]{0:T(128)S(1)} %get-tuple-element.42, f32[2]{0:T(128)S(1)} %get-tuple-element.43, f32[2]{0:T(128)S(1)} %get-tuple-element.44, f32[2]{0:T(128)S(1)} %get-tuple-element.45, f32[2]{0:T(128)S(1)} %get-tuple-element.46, ...), kind=kLoop, calls=%fused_computation.11 | loop fusion | flops 48234496 | bytes 41943104 | tf_op jit(solution)/shard_map/add | solution.py:59
  33.1 3.9 %add_convert_fusion = (bf16[256,1,2,2048]{3,2,1,0:T(2,128)(2,1)S(1)}, bf16[256,1,2,2048]{3,2,1,0:T(2,128)(2,1)S(1)}) fusion(f32[256,2,2,2048]{3,2,1,0:T(2,128)S(1)} %fusion), kind=kLoop, calls=%fused_computation.26 | loop fusion | flops 4194304 | bytes 12582912 | tf_op jit(solution)/shard_map/convert_element_type | solution.py:62
  36.9 0.9 copy.48
  37.8 0.9 copy.49
  38.8 0.8 fusion.7
  39.6 0.8 fusion.15
  40.9 0.7 copy.37
  41.7 7.4 %all-to-all-start = ((f32[16,8,2,256]{3,1,2,0:T(8,128)}), f32[16,8,2,256]{3,1,2,0:T(8,128)S(1)}, u32[]{:S(2)}, u32[]{:S(2)}) async-start(f32[16,8,2,256]{3,1,2,0:T(8,128)} %copy.37), calls=%async_computation | async-start | bytes 524288 | tf_op jit(solution)/shard_map/all_to_all | solution.py:102
  50.3 0.7 fusion.64
  67.8 1.0 gather_fusion.1
  69.1 0.6 pad_select_fusion.9
  69.7 1.0 gather_fusion
  70.7 0.7 select_add_fusion.3
  71.6 1.0 gather_fusion.3
  72.9 0.6 pad_select_fusion.8
  73.5 0.5 pad_select_fusion.7
  74.0 1.0 gather_fusion.2
  75.0 0.8 select_add_fusion.2
  75.9 1.0 gather_fusion.5
  77.1 0.6 pad_select_fusion.6
  77.8 0.5 pad_select_fusion.5
  78.3 0.5 pad_select_fusion.4
  78.8 1.0 gather_fusion.4
  79.8 1.0 select_add_fusion.1
  80.9 1.0 gather_fusion.7
  82.1 0.6 pad_select_fusion.3
  82.8 0.5 pad_select_fusion.2
  83.3 0.5 pad_select_fusion.1
  83.7 0.5 pad_select_fusion
  84.2 1.0 gather_fusion.6
  85.3 0.8 select_add_fusion
  86.1 0.7 gather_fusion.9
  88.4 0.7 gather_fusion.8
  89.5 4.8 %reduce-window.6 = f32[8,64,2,128]{3,1,2,0:T(8,128)S(1)} reduce-window(f32[8,64,2,128]{3,1,2,0:T(8,128)S(1)} %copy.42, f32[]{:T(128)} %constant.60.clone.1), window={size=1x1x1x128 pad=0_0x0_0x0_0x127_0}, to_apply=%region_3.9 | reduce-window | flops 16646144 | bytes 1048580 | tf_op jit(solution)/shard_map/reduce-window
  95.0 1.0 fusion.38
  98.5 0.8 collective-permute-done
  99.3 1.9 %collective-permute-start.1 = (f32[64]{0:T(128)S(1)}, f32[64]{0:T(128)S(1)}, u32[]{:S(2)}, u32[]{:S(2)}) collective-permute-start(f32[64]{0:T(128)S(1)} %max.12), channel_id=1, source_target_pairs={{0,2},{1,3},{2,0},{3,1},{4,6},{5,7},{6,4},{7,5},{8,10},{9,11},{10,... | collective-permute-start | bytes 776 | tf_op jit(solution)/shard_map/ppermute | solution.py:135
  101.1 1.7 %collective-permute-done.1 = f32[64]{0:T(128)S(1)} collective-permute-done((f32[64]{0:T(128)S(1)}, f32[64]{0:T(128)S(1)}, u32[]{:S(2)}, u32[]{:S(2)}) %collective-permute-start.1) | collective-permute-done | bytes 288 | tf_op jit(solution)/shard_map/ppermute | solution.py:135
  102.9 1.9 %collective-permute-start.2 = (f32[64]{0:T(128)S(1)}, f32[64]{0:T(128)S(1)}, u32[]{:S(2)}, u32[]{:S(2)}) collective-permute-start(f32[64]{0:T(128)S(1)} %max.13), channel_id=1, source_target_pairs={{0,4},{1,5},{2,6},{3,7},{4,0},{5,1},{6,2},{7,3},{8,12},{9,13},{10,... | collective-permute-start | bytes 776 | tf_op jit(solution)/shard_map/ppermute | solution.py:135
  104.7 1.0 copy.46
  105.7 0.8 collective-permute-done.2
  106.4 2.8 %collective-permute-start.3 = (f32[64]{0:T(128)S(1)}, f32[64]{0:T(128)S(1)}, u32[]{:S(2)}, u32[]{:S(2)}) collective-permute-start(f32[64]{0:T(128)S(1)} %max.14), channel_id=1, source_target_pairs={{0,8},{1,9},{2,10},{3,11},{4,12},{5,13},{6,14},{7,15},{8,0},{9,1},... | collective-permute-start | bytes 776 | tf_op jit(solution)/shard_map/ppermute | solution.py:135
  109.2 0.7 stack.64
  109.9 1.0 collective-permute-done.3
  110.9 0.5 max.15
  (97 shorter events, 9.0 us)
Async XLA Ops:
  39.6 9.5 %copy-start.1 = (s32[5,2,128]{2,1,0:T(2,128)S(1)}, s32[5,2,128]{2,1,0:T(2,128)}, u32[]{:S(2)}) copy-start(s32[5,2,128]{2,1,0:T(2,128)} %param.18) | copy-start | bytes 15364
  39.6 10.0 %slice-start = ((s32[5,2,128]{2,1,0:T(2,128)}), s32[1,2,128]{2,1,0:T(2,128)S(1)}, s32[]{:S(2)}) async-start(s32[5,2,128]{2,1,0:T(2,128)} %param.18), calls=%async_computation.1 | async-start | bytes 2048 | tf_op jit(solution)/shard_map/slice | solution.py:96
  39.6 10.6 %copy-start = (s32[8]{0:T(128)S(1)}, s32[8]{0:T(128)}, u32[]{:S(2)}) copy-start(s32[8]{0:T(128)} %param.19) | copy-start | bytes 100
  41.7 25.5 %all-to-all-start = ((f32[16,8,2,256]{3,1,2,0:T(8,128)}), f32[16,8,2,256]{3,1,2,0:T(8,128)S(1)}, u32[]{:S(2)}, u32[]{:S(2)}) async-start(f32[16,8,2,256]{3,1,2,0:T(8,128)} %copy.37), calls=%async_computation | async-start | bytes 524288 | tf_op jit(solution)/shard_map/all_to_all | solution.py:102
  98.1 1.2 %collective-permute-start = (f32[64]{0:T(128)S(1)}, f32[64]{0:T(128)S(1)}, u32[]{:S(2)}, u32[]{:S(2)}) collective-permute-start(f32[64]{0:T(128)S(1)} %maximum_dynamic-update-slice_fusion), channel_id=1, source_target_pairs={{0,1},{1,0},{2,3},{3,2},{4,5},{5,4},{6,7},{7,6},{8,9},{9,8},{10,11... | collective-permute-start | bytes 776 | tf_op jit(solution)/shard_map/ppermute | solution.py:135
  99.3 3.6 %collective-permute-start.1 = (f32[64]{0:T(128)S(1)}, f32[64]{0:T(128)S(1)}, u32[]{:S(2)}, u32[]{:S(2)}) collective-permute-start(f32[64]{0:T(128)S(1)} %max.12), channel_id=1, source_target_pairs={{0,2},{1,3},{2,0},{3,1},{4,6},{5,7},{6,4},{7,5},{8,10},{9,11},{10,... | collective-permute-start | bytes 776 | tf_op jit(solution)/shard_map/ppermute | solution.py:135
  102.9 3.6 %collective-permute-start.2 = (f32[64]{0:T(128)S(1)}, f32[64]{0:T(128)S(1)}, u32[]{:S(2)}, u32[]{:S(2)}) collective-permute-start(f32[64]{0:T(128)S(1)} %max.13), channel_id=1, source_target_pairs={{0,4},{1,5},{2,6},{3,7},{4,0},{5,1},{6,2},{7,3},{8,12},{9,13},{10,... | collective-permute-start | bytes 776 | tf_op jit(solution)/shard_map/ppermute | solution.py:135
  106.4 4.5 %collective-permute-start.3 = (f32[64]{0:T(128)S(1)}, f32[64]{0:T(128)S(1)}, u32[]{:S(2)}, u32[]{:S(2)}) collective-permute-start(f32[64]{0:T(128)S(1)} %max.14), channel_id=1, source_target_pairs={{0,8},{1,9},{2,10},{3,11},{4,12},{5,13},{6,14},{7,15},{8,0},{9,1},... | collective-permute-start | bytes 776 | tf_op jit(solution)/shard_map/ppermute | solution.py:135

commit v2 on v0

v2 whole, which is shorter than its diff:
```python
import functools
import math

import jax
import jax.numpy as jnp
from jax import lax
from jax.experimental import pallas as pl
from jax.experimental.pallas import tpu as pltpu
from jax.sharding import PartitionSpec as P


def k1_kernel(chunk, taps_ref, x_hbm, w_hbm, out_ref, slab, wbuf, fine, x_sem, w_sem):
    tap_total, branches = taps_ref.shape
    rows_in, tiles = x_hbm.shape[0], x_hbm.shape[1]
    samples = fine.shape[2]
    beams2 = wbuf.shape[1]
    beams = beams2 // 2
    flat = slab.reshape(tiles, 2 * slab.shape[1], 128)
    window = -(-4 * (chunk + tap_total - 1) // 16) * 16

    def x_copy(j):
        return pltpu.make_async_copy(x_hbm.at[:, j], slab.at[j, pl.ds(0, rows_in)], x_sem.at[j])

    for j in range(tiles):
        x_copy(j).start()
    w_copy = pltpu.make_async_copy(w_hbm, wbuf, w_sem)
    w_copy.start()
    shape = (2, 2, chunk, window)
    col = lax.broadcasted_iota(jnp.int32, shape, 3)
    part = lax.broadcasted_iota(jnp.int32, shape, 0)
    fsel = lax.broadcasted_iota(jnp.int32, shape, 1)
    tap = (col >> 2) - lax.broadcasted_iota(jnp.int32, shape, 2)
    branch = (col >> 1) & 1
    code = jnp.where((col & 1) == part, tap * 2 + branch, -1)
    weights = jnp.zeros(shape, jnp.float32)
    for k in range(tap_total):
        for p in range(branches):
            weights = jnp.where(code == 2 * k + p, taps_ref[k, p], weights)
    weights = jnp.where((fsel & branch) == 1, -weights, weights).reshape(4 * chunk, window)
    high = weights.astype(jnp.bfloat16)
    low = (weights - high.astype(jnp.float32)).astype(jnp.bfloat16)
    both = jnp.concatenate([high, low], 0)
    starts = list(range(0, samples - chunk, chunk)) + [samples - chunk]

    def pair(g, carry):
        x_copy(2 * g).wait()
        x_copy(2 * g + 1).wait()
        for s0 in starts:
            pieces = [flat[2 * g + i, pl.ds(4 * s0, window), :] for i in range(2)]
            got = jnp.dot(both, jnp.concatenate(pieces, 1), preferred_element_type=jnp.float32)
            rounded = (got[: 4 * chunk] + got[4 * chunk :]).astype(jnp.bfloat16)
            for q in range(4):
                fine[q // 2, q % 2, pl.ds(s0, chunk), pl.ds(pl.multiple_of(256 * g, 256), 256)] = rounded[q * chunk : (q + 1) * chunk]
        return carry

    for j in range(tiles):
        spare = slab.shape[1] - rows_in
        if spare:
            slab[j, pl.ds(rows_in, spare)] = jnp.zeros((spare, 2, 128), jnp.bfloat16)
    lax.fori_loop(0, tiles // 2, pair, 0)
    w_copy.wait()
    for f in range(2):
        dims = (((1,), (1,)), ((), ()))
        got_re = lax.dot_general(wbuf[f], fine[0, f], dims, preferred_element_type=jnp.float32)
        got_im = lax.dot_general(wbuf[f], fine[1, f], dims, preferred_element_type=jnp.float32)
        beam_re = got_re[:beams] - got_im[beams:]
        beam_im = got_re[beams:] + got_im[:beams]
        power = beam_re * beam_re + beam_im * beam_im
        level = jnp.mean(power, axis=-1, keepdims=True)
        centered = power - level
        spread = jnp.mean(centered * centered, axis=-1, keepdims=True)
        normed = centered / jnp.sqrt(spread + 1e-05)
        if out_ref.ndim == 5:
            normed = normed.reshape(out_ref.shape[1], out_ref.shape[3], samples)
            for h in range(2):
                out_ref[h, :, f] = normed
        else:
            out_ref[f] = normed

def k1(taps, volume, steering, per):
    t, branches, parts, antennas = volume.shape
    tap_total = taps.shape[0]
    samples = t - tap_total + 1
    beams = steering.shape[-1]
    tiles = antennas // 128
    x = volume.reshape(t * 2, 2, tiles, 128).transpose(0, 2, 1, 3)
    w = steering.transpose(0, 1, 3, 2).reshape(2, 2 * beams, antennas)
    chunk = (64 - tap_total + 1) // 16 * 16
    depth = -(-4 * t // 16) * 16
    out_dims = (2, beams // per, 2, per, samples) if per % 8 == 0 else (2, beams, samples)
    return pl.pallas_call(
        functools.partial(k1_kernel, chunk),
        out_shape=jax.ShapeDtypeStruct(out_dims, jnp.float32),
        in_specs=[
            pl.BlockSpec(memory_space=pltpu.SMEM),
            pl.BlockSpec(memory_space=pltpu.HBM),
            pl.BlockSpec(memory_space=pltpu.HBM),
        ],
        out_specs=pl.BlockSpec(memory_space=pltpu.VMEM),
        scratch_shapes=[
            pltpu.VMEM((tiles, depth // 2, 2, 128), jnp.bfloat16),
            pltpu.VMEM((2, 2 * beams, antennas), jnp.bfloat16),
            pltpu.VMEM((2, 2, samples, antennas), jnp.bfloat16),
            pltpu.SemaphoreType.DMA((tiles,)),
            pltpu.SemaphoreType.DMA,
        ],
        compiler_params=pltpu.CompilerParams(vmem_limit_bytes=50 << 20),
        name="channelize",
    )(taps, x, w)


UNROLL = 32

def shift_static(value, amount):
    rolled = pltpu.roll(value, amount, 1)
    lane = lax.broadcasted_iota(jnp.int32, value.shape, 1)
    return jnp.where(lane >= amount, rolled, 0.0)

def shift_dynamic(value, amount, limit):
    tiles = value.shape[-1] // 128
    pieces = [value[:, 128 * t : 128 * t + 128] for t in range(tiles)]
    lane = lax.broadcasted_iota(jnp.int32, pieces[0].shape, 1)
    zero = jnp.zeros_like(pieces[0])
    rest = amount
    if limit > 128:
        whole = amount >> 7
        rest = amount & 127
        moved = list(pieces)
        for t in range(tiles):
            moved[t] = zero
            for q in range(t + 1):
                moved[t] = jnp.where(whole == q, pieces[t - q], moved[t])
        pieces = moved
    rolled = [pltpu.roll(piece, rest, 1) for piece in pieces]
    kept = lane >= rest
    out = [jnp.where(kept, rolled[t], rolled[t - 1] if t else zero) for t in range(tiles)]
    return jnp.concatenate(out, 1)

def k2_kernel(place_ref, offsets_ref, boxes_ref, normed_ref, dedispersed_ref, scores_ref, peak_ref, planes, other, ramp):
    channels, per, samples = normed_ref.shape
    level_total = offsets_ref.shape[0]
    delays = planes.shape[1]
    rate = delays // channels
    half_rows = delays // 2
    half = place_ref[0]
    block = place_ref[1]
    total = normed_ref[0]
    for c in range(1, channels):
        total = total + normed_ref[c]
    common = total * (1.0 / channels)

    def first(i, carry):
        terms = []
        for u in range(4):
            cleaned = normed_ref[4 * i + u] - common
            terms.append(cleaned)
            for lag in range(1, rate):
                terms.append(terms[-1] + shift_static(cleaned, lag))
        for u in range(4 * rate):
            planes[0, 4 * rate * i + u] = terms[u]
        return carry

    lax.fori_loop(0, channels // 4, first, 0)

    def merged(level, row):
        out_rows = rate << (level + 1)
        child = out_rows // 2
        low = offsets_ref[level, 0, row]
        high = offsets_ref[level, 1, row]
        base = row & ~(out_rows - 1)
        upper = planes[level % 2, base + child + high]
        return planes[level % 2, base + low] + shift_dynamic(upper, low, child)

    for level in range(level_total - 1):
        def one(i, carry, level=level):
            rows = [merged(level, UNROLL * i + u) for u in range(UNROLL)]
            for u in range(UNROLL):
                planes[(level + 1) % 2, UNROLL * i + u] = rows[u]
            return carry
        lax.fori_loop(0, delays // UNROLL, one, 0)

    scale = 1.0 / math.sqrt(channels)
    level = level_total - 1
    for own in range(2):
        start = (half if own == 0 else 1 - half) * half_rows
        target = dedispersed_ref if own == 0 else other
        def last(i, carry, start=start, target=target):
            rows = [merged(level, start + UNROLL * i + u) * scale for u in range(UNROLL)]
            if per % 8 == 0:
                target[:, pl.ds(pl.multiple_of(UNROLL * i, UNROLL), UNROLL), :] = jnp.transpose(jnp.stack(rows, 0), (1, 0, 2))
            else:
                for u in range(UNROLL):
                    for b in range(per):
                        target[b, pl.ds(UNROLL * i + u, 1), :] = rows[u][b : b + 1]
            return carry
        lax.fori_loop(0, half_rows // UNROLL, last, 0)

    width = per * half_rows
    later = lax.broadcasted_iota(jnp.int32, (samples, samples), 0)
    earlier = lax.broadcasted_iota(jnp.int32, (samples, samples), 1)
    upto = jnp.where(earlier <= later, 1.0, 0.0).astype(jnp.bfloat16)
    groups = width // 128
    for g in range(groups):
        ramp[g, pl.ds(0, samples), :] = jnp.zeros((samples, 128), jnp.float32)
    best = None
    for own in range(2):
        source = dedispersed_ref if own == 0 else other
        rest = source[...].reshape(width, samples)
        running = None
        for piece in range(3):
            part = rest.astype(jnp.bfloat16)
            if piece < 2:
                rest = rest - part.astype(jnp.float32)
            got = lax.dot_general(upto, part, (((1,), (1,)), ((), ())), preferred_element_type=jnp.float32)
            running = got if running is None else running + got
        for g in range(groups):
            ramp[g, pl.ds(samples, samples), :] = running[:, 128 * g : 128 * g + 128]
        found = []
        for w in range(boxes_ref.shape[0]):
            length = boxes_ref[w]
            root = jnp.sqrt(jnp.full((1, 128), length, jnp.int32).astype(jnp.float32))
            peaks_here = []
            for g in range(groups):
                response = ramp[g, pl.ds(samples, samples), :] - ramp[g, pl.ds(samples - length, samples), :]
                peaks_here.append(jnp.max(response, axis=0, keepdims=True) / root)
            found.append(jnp.concatenate(peaks_here, 1))
        table = jnp.concatenate(found, 0)
        if own == 0:
            for b in range(per):
                scores_ref[b] = table[:, half_rows * b : half_rows * (b + 1)]
        top = jnp.max(table, axis=0, keepdims=True)
        best = top if best is None else jnp.maximum(best, top)
    lane = lax.broadcasted_iota(jnp.int32, peak_ref.shape, 1)
    peaks = jnp.full(peak_ref.shape, -jnp.inf, jnp.float32)
    for b in range(per):
        one_beam = jnp.max(best[:, half_rows * b : half_rows * (b + 1)], axis=1, keepdims=True)
        peaks = jnp.where(lane == block * per + b, one_beam, peaks)
    peak_ref[...] = peaks

def k2(place, offsets, boxes, normed, beams):
    channels, per, samples = normed.shape
    delays = offsets.shape[-1]
    half_rows = delays // 2
    smem = pl.BlockSpec(memory_space=pltpu.SMEM)
    vmem = pl.BlockSpec(memory_space=pltpu.VMEM)
    return pl.pallas_call(
        k2_kernel,
        out_shape=(
            jax.ShapeDtypeStruct((per, half_rows, samples), jnp.float32),
            jax.ShapeDtypeStruct((per, boxes.shape[0], half_rows), jnp.float32),
            jax.ShapeDtypeStruct((1, beams), jnp.float32),
        ),
        in_specs=[smem, smem, smem, vmem],
        out_specs=(vmem, vmem, vmem),
        scratch_shapes=[
            pltpu.VMEM((2, delays, per, samples), jnp.float32),
            pltpu.VMEM((per, half_rows, samples), jnp.float32),
            pltpu.VMEM((per * half_rows // 128, 2 * samples, 128), jnp.float32),
        ],
        compiler_params=pltpu.CompilerParams(vmem_limit_bytes=50 << 20),
        name="dedisperse",
    )(place, offsets, boxes, normed)


def shards(voltages, pfb_taps, steering, fdmt_offsets, box_lengths):
    devices = lax.axis_size("freq")
    device_id = lax.axis_index("freq")
    beams = steering.shape[-1]
    blocks = devices // 2
    per = beams // blocks
    samples = voltages.shape[1] - pfb_taps.shape[0] + 1
    normed = k1(pfb_taps, voltages[0], steering, per)
    if normed.ndim == 3:
        normed = normed.reshape(2, blocks, per, samples).transpose(1, 0, 2, 3)
        normed = jnp.broadcast_to(normed[None], (2,) + normed.shape)
    outgoing = normed.reshape(devices, 2, per, samples)
    incoming = lax.all_to_all(outgoing, "freq", split_axis=0, concat_axis=0, tiled=True)
    place = jnp.stack([device_id // blocks, device_id % blocks]).astype(jnp.int32)
    dedispersed, box_scores, peaks = k2(
        place, fdmt_offsets, box_lengths, incoming.reshape(2 * devices, per, samples), beams
    )
    step = 1
    while step < blocks:
        pairs = [(spot, spot ^ step) for spot in range(devices)]
        peaks = jnp.maximum(peaks, lax.ppermute(peaks, "freq", pairs))
        step *= 2
    return (dedispersed, box_scores, peaks.reshape(beams))


def solution(mesh):
    placed = (
        P(("groups", "freq"), None, None, None, None),
        P(),
        P(("groups", "freq"), None, None, None),
        P(),
        P(),
    )
    return jax.shard_map(
        shards,
        mesh=mesh,
        in_specs=placed,
        out_specs=(
            P(("groups", "freq"), None, None),
            P(("groups", "freq"), None, None),
            P("groups"),
        ),
        check_vma=False,
    )
```

time: 134 us -> 46.1 us (0.34)
  other arithmetic: 54.1 us -> 0.6 us
  blocking collectives: 34.3 us -> 0 us
  local copies, waits for them, and re-layouts: 19.7 us -> 2 us
  waiting for transfers between devices: 0.01 us -> 17.7 us
  Pallas kernels: 0 us -> 16.9 us
  between operations: 16.8 us -> 0.69 us
  matrix products: 1.67 us -> 0 us
    pmax x1 -> x0, blocking collectives: 34.3 us -> none  [shards(): peak_per_beam = lax.pmax(contrib, 'freq')]
    add x6 -> x0, other arithmetic: 32.3 us -> none  [the longest x1 28.8 us: beam_powers(): filtered + pfb_taps[tap_index][None, :, None, None] * volume[tap_index:ta...]
    pallas_call x0 -> x2, Pallas kernels: none -> 16.9 us  [the longest x1 8.58 us: k1(): pl.pallas_call(functools.partial(k1_kernel, chunk), out_shape=jax.ShapeDt...]
    gather x23 -> x0, local copies, waits for them, and re-layouts: 10.6 us -> none  [take_band(): return jnp.take(band_rows, row_index, axis=0)]
    all_to_all x1, waiting for transfers between devices: 0.01 us -> 9.92 us  [shards(): lax.all_to_all(outgoing, 'freq', split_axis=0, concat_axis=0, tiled=True)]
    select_n x20 -> x0, other arithmetic: 7.75 us -> none  [the longest x15 6.81 us: delay_rows(): jnp.where(chosen[:, :, None, None], shift_time(result, step_size), result)]
    ppermute x0 -> x3, waiting for transfers between devices: none -> 7.74 us  [shards(): peaks = jnp.maximum(peaks, lax.ppermute(peaks, 'freq', pairs))]
    another operation x5 -> x1, other arithmetic: 5.17 us -> 0.08 us  [shards(): jnp.stack([device_id // blocks, device_id % blocks]).astype(jnp.int32)]
  transfers between devices with their start and end apart: 1 -> 4, of which waited for: 0 -> 4; matrix products, arithmetic and copies ran while one was open for 2% -> 0% of each run, Pallas kernels for 0% -> 0%
where the time goes in v2:
time: 46.1 us; the launch traced here: 45.8 us
  waiting for transfers between devices  17.7 us (38%)
  Pallas kernels  16.9 us (37%)
  starting transfers between devices  7.99 us (17%)
  local copies, waits for them, and re-layouts  2 us (4%)
  between operations  0.69 us (1%)
  other arithmetic  0.6 us (1%)
    all_to_all x1, waiting for transfers between devices, shards(): lax.all_to_all(outgoing, 'freq', split_axis=0, concat_axis=0, tiled=True)  9.92 us
    pallas_call x1, Pallas kernels, k1(): pl.pallas_call(functools.partial(k1_kernel, chunk), out_shape=jax.ShapeDt...  8.58 us
    pallas_call x1, Pallas kernels, k2(): pl.pallas_call(k2_kernel, out_shape=(jax.ShapeDtypeStruct((per, half_rows...  8.34 us
    ppermute x3, waiting for transfers between devices, shards(): peaks = jnp.maximum(peaks, lax.ppermute(peaks, 'freq', pairs))  7.74 us
    all_to_all x1, starting transfers between devices, shards(): lax.all_to_all(outgoing, 'freq', split_axis=0, concat_axis=0, tiled=True)  7.43 us
    unnamed x7, local copies, waits for them, and re-layouts  2 us
  transfers between devices with their start and end apart: 4, of which 4 were waited for; matrix products, arithmetic and copies ran while one was open for 0% of the time, Pallas kernels for 0%

profile of v2, /device:TPU:0, one launch (start us, length us, event | category | flops | bytes accessed | tf_op | source)
XLA Modules:
  0.0 45.8 jit_solution(9792552957570627310)
XLA Ops:
  0.6 0.0 copy-start.2
  0.6 0.0 copy-start.1
  0.7 0.8 %copy.8.taps_ref = f32[8,2]{1,0:T(8,128)S(1)} copy(f32[8,2]{0,1:T(2,128)} %param.6) | data formatting | bytes 128 | tf_op args[1]
  1.4 0.0 copy-start
  1.4 1.2 %copy-done = bf16[2,2,2048,64]{2,3,1,0:T(8,128)(2,1)S(1)} copy-done((bf16[2,2,2048,64]{2,3,1,0:T(8,128)(2,1)S(1)}, bf16[2,2,2048,64]{2,3,1,0:T(8,128)(2,1)}, u32[]{:S(2)}) %copy-start) | copy-done | bytes 1048600
  2.6 8.6 %channelize.1 = f32[2,8,2,8,256]{4,3,2,1,0:T(8,128)} custom-call(f32[8,2]{1,0:T(8,128)S(1)} %copy.8.taps_ref, bf16[526,16,2,128]{3,2,1,0:T(2,128)(2,1)} %bitcast.14, bf16[2,128,2048]{2,1,0:T(8,128)(2,1)S(1)} %bitcast.12), custom_call_target="tpu_custom_call" | custom-call | tf_op jit(solution)/shard_map/channelize/pallas_call | solution.py:91
  11.2 7.4 %all-to-all-start = ((f32[16,2,8,256]{3,2,1,0:T(8,128)}), f32[16,2,8,256]{3,2,1,0:T(8,128)S(1)}, u32[]{:S(2)}, u32[]{:S(2)}) async-start(f32[16,2,8,256]{3,2,1,0:T(8,128)} %bitcast.6), calls=%async_computation | async-start | bytes 524288 | tf_op jit(solution)/shard_map/all_to_all | solution.py:277
  18.7 0.1 pad_add_fusion.place_ref
  18.8 9.9 %all-to-all-done = f32[16,2,8,256]{3,2,1,0:T(8,128)S(1)} async-done(((f32[16,2,8,256]{3,2,1,0:T(8,128)}), f32[16,2,8,256]{3,2,1,0:T(8,128)S(1)}, u32[]{:S(2)}, u32[]{:S(2)}) %all-to-all-start) | async-done | bytes 262176 | tf_op jit(solution)/shard_map/all_to_all | solution.py:277
  28.7 0.0 copy-done.2
  28.7 0.0 copy-done.1
  28.7 8.3 %dedisperse.1 = (f32[8,64,256]{2,1,0:T(8,128)}, f32[8,8,64]{2,1,0:T(8,128)}, f32[1,64]{1,0:T(1,128)S(1)}) custom-call(s32[2]{0:T(128)S(1)} %pad_add_fusion.place_ref, s32[5,2,128]{2,1,0:T(2,128)S(1)} %copy-done.1, s32[8]{0:T(128)S(1)} %copy-done.2, f32[32,8,256]{2,1,0:T(8,128)S(1)} %bitcast.13), custom_call_target="tpu_custom_call" | custom-call | tf_op jit(solution)/shard_map/dedisperse/pallas_call | solution.py:246
  37.0 0.0 collective-permute-start
  37.0 1.2 %collective-permute-done = f32[1,64]{1,0:T(1,128)S(1)} collective-permute-done((f32[1,64]{1,0:T(1,128)S(1)}, f32[1,64]{1,0:T(1,128)S(1)}, u32[]{:S(2)}, u32[]{:S(2)}) %collective-permute-start) | collective-permute-done | bytes 288 | tf_op jit(solution)/shard_map/ppermute | solution.py:285
  38.2 0.2 collective-permute-start.1
  38.4 3.4 %collective-permute-done.1 = f32[1,64]{1,0:T(1,128)S(1)} collective-permute-done((f32[1,64]{1,0:T(1,128)S(1)}, f32[1,64]{1,0:T(1,128)S(1)}, u32[]{:S(2)}, u32[]{:S(2)}) %collective-permute-start.1) | collective-permute-done | bytes 288 | tf_op jit(solution)/shard_map/ppermute | solution.py:285
  41.8 0.4 collective-permute-start.2
  42.1 3.2 %collective-permute-done.2 = f32[1,64]{1,0:T(1,128)S(1)} collective-permute-done((f32[1,64]{1,0:T(1,128)S(1)}, f32[1,64]{1,0:T(1,128)S(1)}, u32[]{:S(2)}, u32[]{:S(2)}) %collective-permute-start.2) | collective-permute-done | bytes 288 | tf_op jit(solution)/shard_map/ppermute | solution.py:285
  45.3 0.5 %maximum_bitcast_fusion = f32[64]{0:T(128)} fusion(f32[1,64]{1,0:T(1,128)S(1)} %max.10, f32[1,64]{1,0:T(1,128)S(1)} %collective-permute-done.2), kind=kLoop, calls=%fused_computation.1 | loop fusion | flops 64 | bytes 768 | tf_op jit(solution)/shard_map/reshape | solution.py:287
  (2 shorter events, 0.0 us)
Async XLA Ops:
  0.6 28.1 %copy-start.2 = (s32[8]{0:T(128)S(1)}, s32[8]{0:T(128)}, u32[]{:S(2)}) copy-start(s32[8]{0:T(128)} %boxes_ref.1) | copy-start | bytes 100
  0.6 28.0 %copy-start.1 = (s32[5,2,128]{2,1,0:T(2,128)S(1)}, s32[5,2,128]{2,1,0:T(2,128)}, u32[]{:S(2)}) copy-start(s32[5,2,128]{2,1,0:T(2,128)} %offsets_ref.1) | copy-start | bytes 15364
  1.4 1.2 %copy-start = (bf16[2,2,2048,64]{2,3,1,0:T(8,128)(2,1)S(1)}, bf16[2,2,2048,64]{2,3,1,0:T(8,128)(2,1)}, u32[]{:S(2)}) copy-start(bf16[2,2,2048,64]{2,3,1,0:T(8,128)(2,1)} %param.7) | copy-start | bytes 3145732
  11.2 17.4 %all-to-all-start = ((f32[16,2,8,256]{3,2,1,0:T(8,128)}), f32[16,2,8,256]{3,2,1,0:T(8,128)S(1)}, u32[]{:S(2)}, u32[]{:S(2)}) async-start(f32[16,2,8,256]{3,2,1,0:T(8,128)} %bitcast.6), calls=%async_computation | async-start | bytes 524288 | tf_op jit(solution)/shard_map/all_to_all | solution.py:277
  37.0 1.2 %collective-permute-start = (f32[1,64]{1,0:T(1,128)S(1)}, f32[1,64]{1,0:T(1,128)S(1)}, u32[]{:S(2)}, u32[]{:S(2)}) collective-permute-start(f32[1,64]{1,0:T(1,128)S(1)} %get-tuple-element.8), channel_id=1, source_target_pairs={{0,1},{1,0},{2,3},{3,2},{4,5},{5,4},{6,7},{7,6},{8,9},{9,8},{10,11... | collective-permute-start | bytes 776 | tf_op jit(solution)/shard_map/ppermute | solution.py:285
  38.2 3.6 %collective-permute-start.1 = (f32[1,64]{1,0:T(1,128)S(1)}, f32[1,64]{1,0:T(1,128)S(1)}, u32[]{:S(2)}, u32[]{:S(2)}) collective-permute-start(f32[1,64]{1,0:T(1,128)S(1)} %max.9), channel_id=1, source_target_pairs={{0,2},{1,3},{2,0},{3,1},{4,6},{5,7},{6,4},{7,5},{8,10},{9,11},{10,... | collective-permute-start | bytes 776 | tf_op jit(solution)/shard_map/ppermute | solution.py:285
  41.8 3.6 %collective-permute-start.2 = (f32[1,64]{1,0:T(1,128)S(1)}, f32[1,64]{1,0:T(1,128)S(1)}, u32[]{:S(2)}, u32[]{:S(2)}) collective-permute-start(f32[1,64]{1,0:T(1,128)S(1)} %max.10), channel_id=1, source_target_pairs={{0,4},{1,5},{2,6},{3,7},{4,0},{5,1},{6,2},{7,3},{8,12},{9,13},{10,... | collective-permute-start | bytes 776 | tf_op jit(solution)/shard_map/ppermute | solution.py:285

commit v3 on v2

--- a/solution.py
+++ b/solution.py
@@ -9,8 +9,8 @@
 from jax.sharding import PartitionSpec as P
 
 
-def k1_kernel(chunk, taps_ref, x_hbm, w_hbm, out_ref, slab, wbuf, fine, x_sem, w_sem):
-    tap_total, branches = taps_ref.shape
+def k1_kernel(chunk, taps_hbm, x_hbm, w_hbm, out_ref, slab, wbuf, fine, taps_ref, x_sem, w_sem, taps_sem):
+    branches, tap_total = taps_ref.shape
     rows_in, tiles = x_hbm.shape[0], x_hbm.shape[1]
     samples = fine.shape[2]
     beams2 = wbuf.shape[1]
@@ -21,10 +21,13 @@
     def x_copy(j):
         return pltpu.make_async_copy(x_hbm.at[:, j], slab.at[j, pl.ds(0, rows_in)], x_sem.at[j])
 
+    taps_copy = pltpu.make_async_copy(taps_hbm, taps_ref, taps_sem)
+    taps_copy.start()
     for j in range(tiles):
         x_copy(j).start()
     w_copy = pltpu.make_async_copy(w_hbm, wbuf, w_sem)
     w_copy.start()
+    taps_copy.wait()
     shape = (2, 2, chunk, window)
     col = lax.broadcasted_iota(jnp.int32, shape, 3)
     part = lax.broadcasted_iota(jnp.int32, shape, 0)
@@ -35,7 +38,7 @@
     weights = jnp.zeros(shape, jnp.float32)
     for k in range(tap_total):
         for p in range(branches):
-            weights = jnp.where(code == 2 * k + p, taps_ref[k, p], weights)
+            weights = jnp.where(code == 2 * k + p, taps_ref[p, k], weights)
     weights = jnp.where((fsel & branch) == 1, -weights, weights).reshape(4 * chunk, window)
     high = weights.astype(jnp.bfloat16)
     low = (weights - high.astype(jnp.float32)).astype(jnp.bfloat16)
@@ -91,22 +94,20 @@
     return pl.pallas_call(
         functools.partial(k1_kernel, chunk),
         out_shape=jax.ShapeDtypeStruct(out_dims, jnp.float32),
-        in_specs=[
-            pl.BlockSpec(memory_space=pltpu.SMEM),
-            pl.BlockSpec(memory_space=pltpu.HBM),
-            pl.BlockSpec(memory_space=pltpu.HBM),
-        ],
+        in_specs=[pl.BlockSpec(memory_space=pltpu.HBM)] * 3,
         out_specs=pl.BlockSpec(memory_space=pltpu.VMEM),
         scratch_shapes=[
             pltpu.VMEM((tiles, depth // 2, 2, 128), jnp.bfloat16),
             pltpu.VMEM((2, 2 * beams, antennas), jnp.bfloat16),
             pltpu.VMEM((2, 2, samples, antennas), jnp.bfloat16),
+            pltpu.SMEM((2, tap_total), jnp.float32),
             pltpu.SemaphoreType.DMA((tiles,)),
             pltpu.SemaphoreType.DMA,
+            pltpu.SemaphoreType.DMA,
         ],
-        compiler_params=pltpu.CompilerParams(vmem_limit_bytes=50 << 20),
+        compiler_params=pltpu.CompilerParams(vmem_limit_bytes=67043328),
         name="channelize",
-    )(taps, x, w)
+    )(taps.T, x, w)
 
 
 UNROLL = 32

time: 46.1 us -> 44.9 us (0.974)
  local copies, waits for them, and re-layouts: 2 us -> 1.34 us
  Pallas kernels: 16.9 us -> 16.4 us
    unnamed x7 -> x4, local copies, waits for them, and re-layouts: 2 us -> 1.34 us
    pallas_call x1, Pallas kernels: 8.58 us -> 7.99 us  [k1(): pl.pallas_call(functools.partial(k1_kernel, chunk), out_shape=jax.ShapeDt...]
where the time goes in v3:
time: 44.9 us; the launch traced here: 44.6 us
  waiting for transfers between devices  17.7 us (39%)
  Pallas kernels  16.4 us (37%)
  starting transfers between devices  7.98 us (18%)
  local copies, waits for them, and re-layouts  1.34 us (3%)
  between operations  0.67 us (1%)
  other arithmetic  0.6 us (1%)
    all_to_all x1, waiting for transfers between devices, shards(): lax.all_to_all(outgoing, 'freq', split_axis=0, concat_axis=0, tiled=True)  9.92 us
    pallas_call x1, Pallas kernels, k2(): pl.pallas_call(k2_kernel, out_shape=(jax.ShapeDtypeStruct((per, half_rows...  8.36 us
    pallas_call x1, Pallas kernels, k1(): pl.pallas_call(functools.partial(k1_kernel, chunk), out_shape=jax.ShapeDt...  7.99 us
    ppermute x3, waiting for transfers between devices, shards(): peaks = jnp.maximum(peaks, lax.ppermute(peaks, 'freq', pairs))  7.74 us
    all_to_all x1, starting transfers between devices, shards(): lax.all_to_all(outgoing, 'freq', split_axis=0, concat_axis=0, tiled=True)  7.43 us
    unnamed x4, local copies, waits for them, and re-layouts  1.34 us
  transfers between devices with their start and end apart: 4, of which 4 were waited for; matrix products, arithmetic and copies ran while one was open for 0% of the time, Pallas kernels for 0%

profile of v3, /device:TPU:0, one launch (start us, length us, event | category | flops | bytes accessed | tf_op | source)
XLA Modules:
  0.0 44.6 jit_solution(6604080468832386787)
XLA Ops:
  0.6 8.0 %channelize.1 = f32[2,8,2,8,256]{4,3,2,1,0:T(8,128)} custom-call(f32[2,8]{1,0:T(2,128)} %bitcast.17, bf16[526,16,2,128]{3,2,1,0:T(2,128)(2,1)} %bitcast.14, bf16[2,128,2048]{2,1,0:T(8,128)(2,1)} %bitcast.16), custom_call_target="tpu_custom_call" | custom-call | tf_op jit(solution)/shard_map/channelize/pallas_call | solution.py:94
  8.6 7.4 %all-to-all-start = ((f32[16,2,8,256]{3,2,1,0:T(8,128)}), f32[16,2,8,256]{3,2,1,0:T(8,128)S(1)}, u32[]{:S(2)}, u32[]{:S(2)}) async-start(f32[16,2,8,256]{3,2,1,0:T(8,128)} %bitcast.15), calls=%async_computation | async-start | bytes 524288 | tf_op jit(solution)/shard_map/all_to_all | solution.py:278
  16.1 0.1 pad_add_fusion.place_ref
  16.2 9.9 %all-to-all-done = f32[16,2,8,256]{3,2,1,0:T(8,128)S(1)} async-done(((f32[16,2,8,256]{3,2,1,0:T(8,128)}), f32[16,2,8,256]{3,2,1,0:T(8,128)S(1)}, u32[]{:S(2)}, u32[]{:S(2)}) %all-to-all-start) | async-done | bytes 262176 | tf_op jit(solution)/shard_map/all_to_all | solution.py:278
  26.1 0.0 copy-start
  26.1 0.7 %copy-done = s32[5,2,128]{2,1,0:T(2,128)S(1)} copy-done((s32[5,2,128]{2,1,0:T(2,128)S(1)}, s32[5,2,128]{2,1,0:T(2,128)}, u32[]{:S(2)}) %copy-start) | copy-done | bytes 5144
  26.8 0.0 copy-start.1
  26.8 0.7 %copy-done.1 = s32[8]{0:T(128)S(1)} copy-done((s32[8]{0:T(128)S(1)}, s32[8]{0:T(128)}, u32[]{:S(2)}) %copy-start.1) | copy-done | bytes 56
  27.4 8.4 %dedisperse.1 = (f32[8,64,256]{2,1,0:T(8,128)}, f32[8,8,64]{2,1,0:T(8,128)}, f32[1,64]{1,0:T(1,128)S(1)}) custom-call(s32[2]{0:T(128)S(1)} %pad_add_fusion.place_ref, s32[5,2,128]{2,1,0:T(2,128)S(1)} %copy-done, s32[8]{0:T(128)S(1)} %copy-done.1, f32[32,8,256]{2,1,0:T(8,128)S(1)} %bitcast.13), custom_call_target="tpu_custom_call" | custom-call | tf_op jit(solution)/shard_map/dedisperse/pallas_call | solution.py:247
  35.8 0.0 collective-permute-start
  35.8 1.2 %collective-permute-done = f32[1,64]{1,0:T(1,128)S(1)} collective-permute-done((f32[1,64]{1,0:T(1,128)S(1)}, f32[1,64]{1,0:T(1,128)S(1)}, u32[]{:S(2)}, u32[]{:S(2)}) %collective-permute-start) | collective-permute-done | bytes 288 | tf_op jit(solution)/shard_map/ppermute | solution.py:286
  37.0 0.2 collective-permute-start.1
  37.1 3.4 %collective-permute-done.1 = f32[1,64]{1,0:T(1,128)S(1)} collective-permute-done((f32[1,64]{1,0:T(1,128)S(1)}, f32[1,64]{1,0:T(1,128)S(1)}, u32[]{:S(2)}, u32[]{:S(2)}) %collective-permute-start.1) | collective-permute-done | bytes 288 | tf_op jit(solution)/shard_map/ppermute | solution.py:286
  40.5 0.4 collective-permute-start.2
  40.9 3.2 %collective-permute-done.2 = f32[1,64]{1,0:T(1,128)S(1)} collective-permute-done((f32[1,64]{1,0:T(1,128)S(1)}, f32[1,64]{1,0:T(1,128)S(1)}, u32[]{:S(2)}, u32[]{:S(2)}) %collective-permute-start.2) | collective-permute-done | bytes 288 | tf_op jit(solution)/shard_map/ppermute | solution.py:286
  44.1 0.5 %maximum_bitcast_fusion = f32[64]{0:T(128)} fusion(f32[1,64]{1,0:T(1,128)S(1)} %max.10, f32[1,64]{1,0:T(1,128)S(1)} %collective-permute-done.2), kind=kLoop, calls=%fused_computation.1 | loop fusion | flops 64 | bytes 768 | tf_op jit(solution)/shard_map/reshape | solution.py:288
  (2 shorter events, 0.0 us)
Async XLA Ops:
  8.6 17.4 %all-to-all-start = ((f32[16,2,8,256]{3,2,1,0:T(8,128)}), f32[16,2,8,256]{3,2,1,0:T(8,128)S(1)}, u32[]{:S(2)}, u32[]{:S(2)}) async-start(f32[16,2,8,256]{3,2,1,0:T(8,128)} %bitcast.15), calls=%async_computation | async-start | bytes 524288 | tf_op jit(solution)/shard_map/all_to_all | solution.py:278
  26.1 0.7 %copy-start = (s32[5,2,128]{2,1,0:T(2,128)S(1)}, s32[5,2,128]{2,1,0:T(2,128)}, u32[]{:S(2)}) copy-start(s32[5,2,128]{2,1,0:T(2,128)} %offsets_ref.1) | copy-start | bytes 15364
  26.8 0.7 %copy-start.1 = (s32[8]{0:T(128)S(1)}, s32[8]{0:T(128)}, u32[]{:S(2)}) copy-start(s32[8]{0:T(128)} %boxes_ref.1) | copy-start | bytes 100
  35.8 1.2 %collective-permute-start = (f32[1,64]{1,0:T(1,128)S(1)}, f32[1,64]{1,0:T(1,128)S(1)}, u32[]{:S(2)}, u32[]{:S(2)}) collective-permute-start(f32[1,64]{1,0:T(1,128)S(1)} %get-tuple-element.8), channel_id=1, source_target_pairs={{0,1},{1,0},{2,3},{3,2},{4,5},{5,4},{6,7},{7,6},{8,9},{9,8},{10,11... | collective-permute-start | bytes 776 | tf_op jit(solution)/shard_map/ppermute | solution.py:286
  37.0 3.6 %collective-permute-start.1 = (f32[1,64]{1,0:T(1,128)S(1)}, f32[1,64]{1,0:T(1,128)S(1)}, u32[]{:S(2)}, u32[]{:S(2)}) collective-permute-start(f32[1,64]{1,0:T(1,128)S(1)} %max.9), channel_id=1, source_target_pairs={{0,2},{1,3},{2,0},{3,1},{4,6},{5,7},{6,4},{7,5},{8,10},{9,11},{10,... | collective-permute-start | bytes 776 | tf_op jit(solution)/shard_map/ppermute | solution.py:286
  40.5 3.6 %collective-permute-start.2 = (f32[1,64]{1,0:T(1,128)S(1)}, f32[1,64]{1,0:T(1,128)S(1)}, u32[]{:S(2)}, u32[]{:S(2)}) collective-permute-start(f32[1,64]{1,0:T(1,128)S(1)} %max.10), channel_id=1, source_target_pairs={{0,4},{1,5},{2,6},{3,7},{4,0},{5,1},{6,2},{7,3},{8,12},{9,13},{10,... | collective-permute-start | bytes 776 | tf_op jit(solution)/shard_map/ppermute | solution.py:286

commit v4 on v3

--- a/solution.py
+++ b/solution.py
@@ -110,157 +110,238 @@
     )(taps.T, x, w)
 
 
-UNROLL = 32
-
-def shift_static(value, amount):
-    rolled = pltpu.roll(value, amount, 1)
-    lane = lax.broadcasted_iota(jnp.int32, value.shape, 1)
-    return jnp.where(lane >= amount, rolled, 0.0)
-
-def shift_dynamic(value, amount, limit):
-    tiles = value.shape[-1] // 128
-    pieces = [value[:, 128 * t : 128 * t + 128] for t in range(tiles)]
+UNROLL = 128
+RAMPS = 4
+
+
+def merge_table(offsets, boxes, half, block, per):
+    levels, _, delays = offsets.shape
+    row = jnp.arange(delays, dtype=jnp.int32)
+    parts = []
+    for level in range(levels):
+        child = delays >> (levels - level)
+        base = row & ~(2 * child - 1)
+        low, high = offsets[level, 0], offsets[level, 1]
+        part = jnp.stack([(base + low) * per, (base + child + high) * per, low])
+        if level == levels - 1:
+            near, far = part[:, : delays // 2], part[:, delays // 2 :]
+            part = jnp.where(half == 0, jnp.concatenate([near, far], 1), jnp.concatenate([far, near], 1))
+        parts.append(part)
+    table = jnp.stack(parts).reshape(-1)
+    tail = jnp.concatenate([boxes, jnp.full((1,), block, jnp.int32)])
+    return jnp.concatenate([table, jnp.pad(tail, (0, 128 - tail.shape[0]))])
+
+
+def repeat(count, body):
+    if count == 1:
+        body(0, 0)
+    else:
+        lax.fori_loop(0, count, body, 0)
+
+
+def split_lanes(value):
+    return [value[:, 128 * t : 128 * t + 128] for t in range(value.shape[-1] // 128)]
+
+
+def shifted(pieces, amount, limit):
     lane = lax.broadcasted_iota(jnp.int32, pieces[0].shape, 1)
     zero = jnp.zeros_like(pieces[0])
+    tiles = len(pieces)
     rest = amount
     if limit > 128:
         whole = amount >> 7
         rest = amount & 127
-        moved = list(pieces)
+        moved = []
         for t in range(tiles):
-            moved[t] = zero
+            piece = zero
             for q in range(t + 1):
-                moved[t] = jnp.where(whole == q, pieces[t - q], moved[t])
+                piece = jnp.where(whole == q, pieces[t - q], piece)
+            moved.append(piece)
         pieces = moved
     rolled = [pltpu.roll(piece, rest, 1) for piece in pieces]
     kept = lane >= rest
-    out = [jnp.where(kept, rolled[t], rolled[t - 1] if t else zero) for t in range(tiles)]
-    return jnp.concatenate(out, 1)
-
-def k2_kernel(place_ref, offsets_ref, boxes_ref, normed_ref, dedispersed_ref, scores_ref, peak_ref, planes, other, ramp):
+    return [jnp.where(kept, rolled[t], rolled[t - 1] if t else zero) for t in range(tiles)]
+
+
+def k2_kernel(
+    table_hbm, normed_ref, dedispersed_ref, scores_ref, peak_ref,
+    plane_a, plane_b, own, other, *rest_refs,
+):
+    *ramps, tops, table_ref, table_sem, out_sem = rest_refs
+    planes = (plane_a, plane_b)
     channels, per, samples = normed_ref.shape
-    level_total = offsets_ref.shape[0]
-    delays = planes.shape[1]
+    delays = plane_a.shape[1] // per
+    tiles = samples // 128
     rate = delays // channels
+    levels = (table_ref.shape[0] - 128) // (3 * delays)
     half_rows = delays // 2
-    half = place_ref[0]
-    block = place_ref[1]
+    box_total = scores_ref.shape[0]
+    tail = 3 * delays * levels
+    table_copy = pltpu.make_async_copy(table_hbm, table_ref, table_sem)
+    table_copy.start()
+    for ramp in ramps:
+        ramp[pl.ds(0, samples), :] = jnp.zeros((samples, 128), jnp.float32)
     total = normed_ref[0]
     for c in range(1, channels):
         total = total + normed_ref[c]
     common = total * (1.0 / channels)
 
+    group = min(4, channels)
+
+    def put(level, t, row, value):
+        rows = pl.ds(row * per if isinstance(row, int) else pl.multiple_of(row * per, per), per)
+        planes[level % 2][t, rows, :] = value
+
     def first(i, carry):
         terms = []
-        for u in range(4):
-            cleaned = normed_ref[4 * i + u] - common
-            terms.append(cleaned)
+        for u in range(group):
+            cleaned = split_lanes(normed_ref[group * i + u] - common)
+            running = cleaned
+            terms.append(running)
             for lag in range(1, rate):
-                terms.append(terms[-1] + shift_static(cleaned, lag))
-        for u in range(4 * rate):
-            planes[0, 4 * rate * i + u] = terms[u]
+                running = [a + b for a, b in zip(running, shifted(cleaned, lag, 1))]
+                terms.append(running)
+        for u in range(group * rate):
+            for t in range(tiles):
+                put(0, t, group * rate * i + u, terms[u][t])
         return carry
 
-    lax.fori_loop(0, channels // 4, first, 0)
+    lax.fori_loop(0, channels // group, first, 0)
+    table_copy.wait()
 
     def merged(level, row):
-        out_rows = rate << (level + 1)
-        child = out_rows // 2
-        low = offsets_ref[level, 0, row]
-        high = offsets_ref[level, 1, row]
-        base = row & ~(out_rows - 1)
-        upper = planes[level % 2, base + child + high]
-        return planes[level % 2, base + low] + shift_dynamic(upper, low, child)
-
-    for level in range(level_total - 1):
+        start = 3 * delays * level
+        lower = table_ref[start + row]
+        upper = table_ref[start + delays + row]
+        low = table_ref[start + 2 * delays + row]
+        source = planes[level % 2]
+        lower_rows = pl.ds(pl.multiple_of(lower, per), per)
+        upper_rows = pl.ds(pl.multiple_of(upper, per), per)
+        moved = shifted([source[t, upper_rows, :] for t in range(tiles)], low, rate << level)
+        return [source[t, lower_rows, :] + moved[t] for t in range(tiles)]
+
+    for level in range(levels - 1):
         def one(i, carry, level=level):
-            rows = [merged(level, UNROLL * i + u) for u in range(UNROLL)]
             for u in range(UNROLL):
-                planes[(level + 1) % 2, UNROLL * i + u] = rows[u]
+                row = merged(level, UNROLL * i + u)
+                for t in range(tiles):
+                    put(level + 1, t, UNROLL * i + u, row[t])
             return carry
-        lax.fori_loop(0, delays // UNROLL, one, 0)
+        repeat(delays // UNROLL, one)
 
     scale = 1.0 / math.sqrt(channels)
-    level = level_total - 1
-    for own in range(2):
-        start = (half if own == 0 else 1 - half) * half_rows
-        target = dedispersed_ref if own == 0 else other
-        def last(i, carry, start=start, target=target):
-            rows = [merged(level, start + UNROLL * i + u) * scale for u in range(UNROLL)]
-            if per % 8 == 0:
-                target[:, pl.ds(pl.multiple_of(UNROLL * i, UNROLL), UNROLL), :] = jnp.transpose(jnp.stack(rows, 0), (1, 0, 2))
-            else:
-                for u in range(UNROLL):
-                    for b in range(per):
-                        target[b, pl.ds(UNROLL * i + u, 1), :] = rows[u][b : b + 1]
+    step = 8
+    span = min(UNROLL, half_rows)
+    for k in range(2):
+        target = own if k == 0 else other
+        def last(i, carry, k=k, target=target):
+            for v in range(span // step):
+                place = span * i + step * v
+                rows = [jnp.concatenate(merged(levels - 1, k * half_rows + place + u), 1) * scale for u in range(step)]
+                if per % 8 == 0:
+                    target[:, pl.ds(place if isinstance(place, int) else pl.multiple_of(place, step), step), :] = jnp.transpose(jnp.stack(rows, 0), (1, 0, 2))
+                else:
+                    for u in range(step):
+                        for b in range(per):
+                            target[b, pl.ds(place + u, 1), :] = rows[u][b : b + 1]
             return carry
-        lax.fori_loop(0, half_rows // UNROLL, last, 0)
-
+        repeat(half_rows // span, last)
+
+    out_copy = pltpu.make_async_copy(own, dedispersed_ref, out_sem)
+    out_copy.start()
     width = per * half_rows
-    later = lax.broadcasted_iota(jnp.int32, (samples, samples), 0)
-    earlier = lax.broadcasted_iota(jnp.int32, (samples, samples), 1)
+    groups = width // 128
+    head = samples // 2
+    later = lax.broadcasted_iota(jnp.int32, (head, head), 0)
+    earlier = lax.broadcasted_iota(jnp.int32, (head, head), 1)
     upto = jnp.where(earlier <= later, 1.0, 0.0).astype(jnp.bfloat16)
-    groups = width // 128
-    for g in range(groups):
-        ramp[g, pl.ds(0, samples), :] = jnp.zeros((samples, 128), jnp.float32)
-    best = None
-    for own in range(2):
-        source = dedispersed_ref if own == 0 else other
-        rest = source[...].reshape(width, samples)
-        running = None
+    upto = jnp.concatenate([upto] * 3, 1)
+    spot = lax.broadcasted_iota(jnp.int32, (box_total, 128), 0)
+    lengths = jnp.zeros((box_total, 128), jnp.int32)
+    for w in range(box_total):
+        lengths = jnp.where(spot == w, table_ref[tail + w], lengths)
+    roots = jnp.sqrt(lengths.astype(jnp.float32))
+    flat = [own.reshape(width, samples), other.reshape(width, samples)]
+    block_rows = 64
+
+    def sums(g, k):
+        rows = flat[k][pl.ds(128 * g, 128), :]
+        rest = jnp.concatenate([rows[:, :head], rows[:, head:]], 0)
+        parts = []
         for piece in range(3):
-            part = rest.astype(jnp.bfloat16)
+            parts.append(rest.astype(jnp.bfloat16))
             if piece < 2:
-                rest = rest - part.astype(jnp.float32)
-            got = lax.dot_general(upto, part, (((1,), (1,)), ((), ())), preferred_element_type=jnp.float32)
-            running = got if running is None else running + got
-        for g in range(groups):
-            ramp[g, pl.ds(samples, samples), :] = running[:, 128 * g : 128 * g + 128]
-        found = []
-        for w in range(boxes_ref.shape[0]):
-            length = boxes_ref[w]
-            root = jnp.sqrt(jnp.full((1, 128), length, jnp.int32).astype(jnp.float32))
-            peaks_here = []
-            for g in range(groups):
-                response = ramp[g, pl.ds(samples, samples), :] - ramp[g, pl.ds(samples - length, samples), :]
-                peaks_here.append(jnp.max(response, axis=0, keepdims=True) / root)
-            found.append(jnp.concatenate(peaks_here, 1))
-        table = jnp.concatenate(found, 0)
-        if own == 0:
-            for b in range(per):
-                scores_ref[b] = table[:, half_rows * b : half_rows * (b + 1)]
-        top = jnp.max(table, axis=0, keepdims=True)
-        best = top if best is None else jnp.maximum(best, top)
-    lane = lax.broadcasted_iota(jnp.int32, peak_ref.shape, 1)
-    peaks = jnp.full(peak_ref.shape, -jnp.inf, jnp.float32)
-    for b in range(per):
-        one_beam = jnp.max(best[:, half_rows * b : half_rows * (b + 1)], axis=1, keepdims=True)
-        peaks = jnp.where(lane == block * per + b, one_beam, peaks)
-    peak_ref[...] = peaks
-
-def k2(place, offsets, boxes, normed, beams):
+                rest = rest - parts[-1].astype(jnp.float32)
+        got = lax.dot_general(
+            upto, jnp.concatenate(parts, 1), (((1,), (1,)), ((), ())), preferred_element_type=jnp.float32
+        )
+        ramp = ramps[(2 * g + k) % len(ramps)]
+        ramp[pl.ds(samples, head), :] = got[:, :128]
+        ramp[pl.ds(samples + head, head), :] = got[:, 128:] + got[head - 1 :, :128]
+
+    def boxes(g, k):
+        ramp = ramps[(2 * g + k) % len(ramps)]
+        best = [None] * box_total
+        for s0 in range(0, samples, block_rows):
+            here = ramp[pl.ds(samples + s0, block_rows), :]
+            for w in range(box_total):
+                response = here - ramp[pl.ds(samples + s0 - table_ref[tail + w], block_rows), :]
+                found = jnp.max(response.reshape(block_rows // 8, 8, 128), axis=0)
+                best[w] = found if best[w] is None else jnp.maximum(best[w], found)
+        scores = jnp.concatenate([jnp.max(b, axis=0, keepdims=True) for b in best], 0) / roots
+        if k == 0:
+            scores_ref[:, pl.ds(128 * g, 128)] = scores
+        tops[pl.ds(k * groups + g, 1), :] = jnp.max(scores, axis=0, keepdims=True)
+
+    order = [(g, k) for k in range(2) for g in range(groups)]
+    sums(*order[0])
+    for n, spot_now in enumerate(order):
+        if n + 1 < len(order):
+            sums(*order[n + 1])
+        boxes(*spot_now)
+    block = table_ref[tail + box_total]
+    values = tops[...]
+    lane = lax.broadcasted_iota(jnp.int32, values.shape, 1)
+    place = lax.broadcasted_iota(jnp.int32, values.shape, 0)
+    place = 128 * jnp.where(place >= groups, place - groups, place)
+    peaks = jnp.full(values.shape, -jnp.inf, jnp.float32)
+    span = min(half_rows, 128)
+    for q in range(128 // span):
+        inside = (lane >= span * q) & (lane < span * (q + 1))
+        top = jnp.max(jnp.where(inside, values, -jnp.inf), axis=1, keepdims=True)
+        beam = block * per + (place + span * q) // half_rows
+        peaks = jnp.where(lane == beam, jnp.maximum(top, peaks), peaks)
+    peak_ref[...] = jnp.max(peaks, axis=0, keepdims=True)[:, : peak_ref.shape[1]]
+    out_copy.wait()
+
+
+def k2(table, normed, beams, delays, box_total):
     channels, per, samples = normed.shape
-    delays = offsets.shape[-1]
     half_rows = delays // 2
-    smem = pl.BlockSpec(memory_space=pltpu.SMEM)
+    groups = per * half_rows // 128
     vmem = pl.BlockSpec(memory_space=pltpu.VMEM)
+    hbm = pl.BlockSpec(memory_space=pl.ANY)
     return pl.pallas_call(
         k2_kernel,
         out_shape=(
             jax.ShapeDtypeStruct((per, half_rows, samples), jnp.float32),
-            jax.ShapeDtypeStruct((per, boxes.shape[0], half_rows), jnp.float32),
+            jax.ShapeDtypeStruct((box_total, per * half_rows), jnp.float32),
             jax.ShapeDtypeStruct((1, beams), jnp.float32),
         ),
-        in_specs=[smem, smem, smem, vmem],
-        out_specs=(vmem, vmem, vmem),
+        in_specs=[hbm, vmem],
+        out_specs=(hbm, vmem, vmem),
         scratch_shapes=[
-            pltpu.VMEM((2, delays, per, samples), jnp.float32),
-            pltpu.VMEM((per, half_rows, samples), jnp.float32),
-            pltpu.VMEM((per * half_rows // 128, 2 * samples, 128), jnp.float32),
+            *[pltpu.VMEM((samples // 128, delays * per, 128), jnp.float32)] * 2,
+            *[pltpu.VMEM((per, half_rows, samples), jnp.float32)] * 2,
+            *[pltpu.VMEM((2 * samples, 128), jnp.float32)] * RAMPS,
+            pltpu.VMEM((2 * groups, 128), jnp.float32),
+            pltpu.SMEM(table.shape, jnp.int32),
+            pltpu.SemaphoreType.DMA,
+            pltpu.SemaphoreType.DMA,
         ],
-        compiler_params=pltpu.CompilerParams(vmem_limit_bytes=50 << 20),
+        compiler_params=pltpu.CompilerParams(vmem_limit_bytes=48 << 20),
         name="dedisperse",
-    )(place, offsets, boxes, normed)
+    )(table, normed)
 
 
 def shards(voltages, pfb_taps, steering, fdmt_offsets, box_lengths):
@@ -276,10 +357,12 @@
         normed = jnp.broadcast_to(normed[None], (2,) + normed.shape)
     outgoing = normed.reshape(devices, 2, per, samples)
     incoming = lax.all_to_all(outgoing, "freq", split_axis=0, concat_axis=0, tiled=True)
-    place = jnp.stack([device_id // blocks, device_id % blocks]).astype(jnp.int32)
+    table = merge_table(fdmt_offsets, box_lengths, device_id // blocks, device_id % blocks, per)
+    delays, box_total = fdmt_offsets.shape[-1], box_lengths.shape[0]
     dedispersed, box_scores, peaks = k2(
-        place, fdmt_offsets, box_lengths, incoming.reshape(2 * devices, per, samples), beams
+        table, incoming.reshape(2 * devices, per, samples), beams, delays, box_total
     )
+    box_scores = box_scores.reshape(box_total, per, delays // 2).transpose(1, 0, 2)
     step = 1
     while step < blocks:
         pairs = [(spot, spot ^ step) for spot in range(devices)]

time: 44.9 us -> 40.3 us (0.90)
  Pallas kernels: 16.4 us -> 13 us
  waiting for transfers between devices: 17.7 us -> 14.4 us
  other arithmetic: 0.6 us -> 3 us
  local copies, waits for them, and re-layouts: 1.34 us -> 0.78 us
    pallas_call x1, Pallas kernels: 8.36 us -> 5 us  [k2(): pl.pallas_call(k2_kernel, out_shape=(jax.ShapeDtypeStruct((per, half_rows...]
    all_to_all x1, waiting for transfers between devices: 9.92 us -> 7.41 us  [shards(): lax.all_to_all(outgoing, 'freq', split_axis=0, concat_axis=0, tiled=True)]
    unnamed x4 -> x0, local copies, waits for them, and re-layouts: 1.34 us -> none
    mul x0 -> x1, other arithmetic: none -> 0.82 us  [merge_table(): part = jnp.stack([(base + low) * per, (base + child + high) * per, low])]
    squeeze x0 -> x1, other arithmetic: none -> 0.77 us  [merge_table(): low, high = (offsets[level, 0], offsets[level, 1])]
    concatenate x0 -> x2, other arithmetic: none -> 0.74 us  [the longest x1 0.73 us: merge_table(): tail = jnp.concatenate([boxes, jnp.full((1,), block, jnp.int32)])]
    reshape x0 -> x3, local copies, waits for them, and re-layouts: none -> 0.71 us  [the longest x2 0.7 us: shards(): box_scores.reshape(box_total, per, delays // 2).transpose(1, 0, 2)]
    ppermute x3, waiting for transfers between devices: 7.74 us -> 7.03 us  [shards(): peaks = jnp.maximum(peaks, lax.ppermute(peaks, 'freq', pairs))]
  transfers between devices with their start and end apart: 4 -> 4, of which waited for: 4 -> 4; matrix products, arithmetic and copies ran while one was open for 0% -> 8% of each run, Pallas kernels for 0% -> 0%
where the time goes in v4:
time: 40.3 us; the launch traced here: 40 us
  waiting for transfers between devices  14.4 us (36%)
  Pallas kernels  13 us (32%)
  starting transfers between devices  8.05 us (20%)
  other arithmetic  3 us (7%)
  local copies, waits for them, and re-layouts  0.78 us (2%)
  between operations  0.7 us (2%)
    pallas_call x1, Pallas kernels, k1(): pl.pallas_call(functools.partial(k1_kernel, chunk), out_shape=jax.ShapeDt...  7.99 us
    all_to_all x1, starting transfers between devices, shards(): lax.all_to_all(outgoing, 'freq', split_axis=0, concat_axis=0, tiled=True)  7.43 us
    all_to_all x1, waiting for transfers between devices, shards(): lax.all_to_all(outgoing, 'freq', split_axis=0, concat_axis=0, tiled=True)  7.41 us
    ppermute x3, waiting for transfers between devices, shards(): peaks = jnp.maximum(peaks, lax.ppermute(peaks, 'freq', pairs))  7.03 us
    pallas_call x1, Pallas kernels, k2(): pl.pallas_call(k2_kernel, out_shape=(jax.ShapeDtypeStruct((per, half_rows...  5 us
    mul x1, other arithmetic, merge_table(): part = jnp.stack([(base + low) * per, (base + child + high) * per, low])  0.82 us
  transfers between devices with their start and end apart: 4, of which 4 were waited for; matrix products, arithmetic and copies ran while one was open for 8% of the time, Pallas kernels for 0%

profile of v4, /device:TPU:0, one launch (start us, length us, event | category | flops | bytes accessed | tf_op | source)
XLA Modules:
  0.0 40.0 jit_solution(16176193047580422221)
XLA Ops:
  0.6 8.0 %channelize.1 = f32[2,8,2,8,256]{4,3,2,1,0:T(8,128)} custom-call(f32[2,8]{1,0:T(2,128)} %bitcast.79, bf16[526,16,2,128]{3,2,1,0:T(2,128)(2,1)} %bitcast.75, bf16[2,128,2048]{2,1,0:T(8,128)(2,1)} %bitcast.77), custom_call_target="tpu_custom_call" | custom-call | tf_op jit(solution)/shard_map/channelize/pallas_call | solution.py:94
  8.6 7.4 %all-to-all-start = ((f32[16,2,8,256]{3,2,1,0:T(8,128)}), f32[16,2,8,256]{3,2,1,0:T(8,128)S(1)}, u32[]{:S(2)}, u32[]{:S(2)}) async-start(f32[16,2,8,256]{3,2,1,0:T(8,128)} %bitcast.76), calls=%async_computation | async-start | bytes 524288 | tf_op jit(solution)/shard_map/all_to_all | solution.py:359
  16.1 0.8 %slice_bitcast_fusion.6 = (s32[1,128]{1,0:T(1,128)S(1)}, s32[1,1,128]{2,1,0:T(1,128)S(1)}, s32[1,128]{1,0:T(1,128)S(1)}, s32[1,128]{1,0:T(1,128)S(1)}, s32[1,128...) fusion(s32[5,2,128]{2,1,0:T(2,128)} %param.8), kind=kLoop, calls=%fused_computation.44 | loop fusion | flops 768 | bytes 7168 | tf_op jit(solution)/shard_map/squeeze | solution.py:124
  16.8 0.8 %add_multiply_fusion = (s32[1,128]{1,0:T(1,128)S(1)}, s32[1,128]{1,0:T(1,128)S(1)}, s32[1,128]{1,0:T(1,128)S(1)}, s32[1,128]{1,0:T(1,128)S(1)}, s32[1,128]{1,0:T...) fusion(s32[5,2,128]{2,1,0:T(2,128)} %param.8), kind=kLoop, calls=%fused_computation.27 | loop fusion | flops 3840 | bytes 10240 | tf_op jit(solution)/shard_map/mul | solution.py:125
  17.7 0.1 slice_bitcast_fusion.1
  17.8 0.1 constant_dynamic-update-slice_fusion
  17.9 0.7 %pad_add_fusion.2 = s32[9]{0:T(128)S(1)} fusion(s32[1]{0:T(128)} %bitcast.16, s32[8]{0:T(128)} %param.9), kind=kLoop, calls=%fused_computation.15 | loop fusion | flops 9 | bytes 72 | tf_op jit(solution)/shard_map/concatenate | solution.py:131
  18.7 7.4 %all-to-all-done = f32[16,2,8,256]{3,2,1,0:T(8,128)S(1)} async-done(((f32[16,2,8,256]{3,2,1,0:T(8,128)}), f32[16,2,8,256]{3,2,1,0:T(8,128)S(1)}, u32[]{:S(2)}, u32[]{:S(2)}) %all-to-all-start) | async-done | bytes 262176 | tf_op jit(solution)/shard_map/all_to_all | solution.py:359
  26.1 5.0 %dedisperse.1 = (f32[8,64,256]{2,1,0:T(8,128)}, f32[8,512]{1,0:T(8,128)S(1)}, f32[1,64]{1,0:T(1,128)S(1)}) custom-call(s32[2048]{0:T(1024)S(1)} %pad_add_fusion.table_hbm, f32[32,8,256]{2,1,0:T(8,128)S(1)} %bitcast.74), custom_call_target="tpu_custom_call" | custom-call | tf_op jit(solution)/shard_map/dedisperse/pallas_call | solution.py:324
  31.1 0.1 collective-permute-start
  31.2 1.1 %collective-permute-done = f32[1,64]{1,0:T(1,128)S(1)} collective-permute-done((f32[1,64]{1,0:T(1,128)S(1)}, f32[1,64]{1,0:T(1,128)S(1)}, u32[]{:S(2)}, u32[]{:S(2)}) %collective-permute-start) | collective-permute-done | bytes 288 | tf_op jit(solution)/shard_map/ppermute | solution.py:369
  32.3 0.2 collective-permute-start.1
  32.5 3.4 %collective-permute-done.1 = f32[1,64]{1,0:T(1,128)S(1)} collective-permute-done((f32[1,64]{1,0:T(1,128)S(1)}, f32[1,64]{1,0:T(1,128)S(1)}, u32[]{:S(2)}, u32[]{:S(2)}) %collective-permute-start.1) | collective-permute-done | bytes 288 | tf_op jit(solution)/shard_map/ppermute | solution.py:369
  35.9 0.4 collective-permute-start.2
  36.3 0.1 reshape.260
  36.3 0.6 %copy.10 = f32[8,8,64]{2,0,1:T(8,128)} copy(f32[8,8,64]{2,1,0:T(8,128)S(1)} %reshape.260) | data formatting | bytes 32768 | tf_op jit(solution)/shard_map/reshape | solution.py:365
  37.0 2.5 %collective-permute-done.2 = f32[1,64]{1,0:T(1,128)S(1)} collective-permute-done((f32[1,64]{1,0:T(1,128)S(1)}, f32[1,64]{1,0:T(1,128)S(1)}, u32[]{:S(2)}, u32[]{:S(2)}) %collective-permute-start.2) | collective-permute-done | bytes 288 | tf_op jit(solution)/shard_map/ppermute | solution.py:369
  39.5 0.5 %maximum_bitcast_fusion = f32[64]{0:T(128)} fusion(f32[1,64]{1,0:T(1,128)S(1)} %max.10, f32[1,64]{1,0:T(1,128)S(1)} %collective-permute-done.2), kind=kLoop, calls=%fused_computation.26 | loop fusion | flops 64 | bytes 768 | tf_op jit(solution)/shard_map/reshape | solution.py:371
  (9 shorter events, 0.1 us)
Async XLA Ops:
  8.6 17.4 %all-to-all-start = ((f32[16,2,8,256]{3,2,1,0:T(8,128)}), f32[16,2,8,256]{3,2,1,0:T(8,128)S(1)}, u32[]{:S(2)}, u32[]{:S(2)}) async-start(f32[16,2,8,256]{3,2,1,0:T(8,128)} %bitcast.76), calls=%async_computation | async-start | bytes 524288 | tf_op jit(solution)/shard_map/all_to_all | solution.py:359
  31.1 1.2 %collective-permute-start = (f32[1,64]{1,0:T(1,128)S(1)}, f32[1,64]{1,0:T(1,128)S(1)}, u32[]{:S(2)}, u32[]{:S(2)}) collective-permute-start(f32[1,64]{1,0:T(1,128)S(1)} %get-tuple-element.8), channel_id=1, source_target_pairs={{0,1},{1,0},{2,3},{3,2},{4,5},{5,4},{6,7},{7,6},{8,9},{9,8},{10,11... | collective-permute-start | bytes 776 | tf_op jit(solution)/shard_map/ppermute | solution.py:369
  32.3 3.6 %collective-permute-start.1 = (f32[1,64]{1,0:T(1,128)S(1)}, f32[1,64]{1,0:T(1,128)S(1)}, u32[]{:S(2)}, u32[]{:S(2)}) collective-permute-start(f32[1,64]{1,0:T(1,128)S(1)} %max.9), channel_id=1, source_target_pairs={{0,2},{1,3},{2,0},{3,1},{4,6},{5,7},{6,4},{7,5},{8,10},{9,11},{10,... | collective-permute-start | bytes 776 | tf_op jit(solution)/shard_map/ppermute | solution.py:369
  35.9 3.6 %collective-permute-start.2 = (f32[1,64]{1,0:T(1,128)S(1)}, f32[1,64]{1,0:T(1,128)S(1)}, u32[]{:S(2)}, u32[]{:S(2)}) collective-permute-start(f32[1,64]{1,0:T(1,128)S(1)} %max.10), channel_id=1, source_target_pairs={{0,4},{1,5},{2,6},{3,7},{4,0},{5,1},{6,2},{7,3},{8,12},{9,13},{10,... | collective-permute-start | bytes 776 | tf_op jit(solution)/shard_map/ppermute | solution.py:369

commit v5 on v4

--- a/solution.py
+++ b/solution.py
@@ -8,6 +8,8 @@
 from jax.experimental.pallas import tpu as pltpu
 from jax.sharding import PartitionSpec as P
 
+
+PAIRS = 4
 
 def k1_kernel(chunk, taps_hbm, x_hbm, w_hbm, out_ref, slab, wbuf, fine, taps_ref, x_sem, w_sem, taps_sem):
     branches, tap_total = taps_ref.shape
@@ -42,30 +44,50 @@
     weights = jnp.where((fsel & branch) == 1, -weights, weights).reshape(4 * chunk, window)
     high = weights.astype(jnp.bfloat16)
     low = (weights - high.astype(jnp.float32)).astype(jnp.bfloat16)
-    both = jnp.concatenate([high, low], 0)
-    starts = list(range(0, samples - chunk, chunk)) + [samples - chunk]
-
-    def pair(g, carry):
-        x_copy(2 * g).wait()
-        x_copy(2 * g + 1).wait()
-        for s0 in starts:
-            pieces = [flat[2 * g + i, pl.ds(4 * s0, window), :] for i in range(2)]
-            got = jnp.dot(both, jnp.concatenate(pieces, 1), preferred_element_type=jnp.float32)
-            rounded = (got[: 4 * chunk] + got[4 * chunk :]).astype(jnp.bfloat16)
+    spans = [(s0, min(chunk, samples - s0)) for s0 in range(0, samples, chunk)]
+    spans = [(s0, size, -(-4 * (size + tap_total - 1) // 16) * 16) for s0, size in spans]
+    filters = {}
+    for _, size, reach in spans:
+        if size not in filters:
+            filters[size] = jnp.concatenate(
+                [part[q * chunk : q * chunk + size, :reach] for part in (high, low) for q in range(4)], 0
+            )
+
+    def load(g, s0, size, reach):
+        pieces = [flat[2 * g + i, pl.ds(4 * s0, reach), :] for i in range(2)]
+        return jnp.concatenate(pieces, 1)
+
+    def pairs(h, carry):
+        work = []
+        for u in range(PAIRS):
+            g = PAIRS * h + u
+            work += [(g, *span) for span in spans]
+        for u in range(PAIRS):
+            x_copy(2 * (PAIRS * h + u)).wait()
+            x_copy(2 * (PAIRS * h + u) + 1).wait()
+        ahead = load(*work[0])
+        for n, (g, s0, size, _) in enumerate(work):
+            here = ahead
+            if n + 1 < len(work):
+                ahead = load(*work[n + 1])
+            got = jnp.dot(filters[size], here, preferred_element_type=jnp.float32)
+            rounded = (got[: 4 * size] + got[4 * size :]).astype(jnp.bfloat16)
             for q in range(4):
-                fine[q // 2, q % 2, pl.ds(s0, chunk), pl.ds(pl.multiple_of(256 * g, 256), 256)] = rounded[q * chunk : (q + 1) * chunk]
+                fine[q // 2, q % 2, pl.ds(s0, size), pl.ds(pl.multiple_of(256 * g, 256), 256)] = rounded[
+                    q * size : (q + 1) * size
+                ]
         return carry
 
     for j in range(tiles):
         spare = slab.shape[1] - rows_in
         if spare:
             slab[j, pl.ds(rows_in, spare)] = jnp.zeros((spare, 2, 128), jnp.bfloat16)
-    lax.fori_loop(0, tiles // 2, pair, 0)
+    lax.fori_loop(0, tiles // 2 // PAIRS, pairs, 0)
     w_copy.wait()
     for f in range(2):
         dims = (((1,), (1,)), ((), ()))
-        got_re = lax.dot_general(wbuf[f], fine[0, f], dims, preferred_element_type=jnp.float32)
-        got_im = lax.dot_general(wbuf[f], fine[1, f], dims, preferred_element_type=jnp.float32)
+        got_re = lax.dot_general(fine[0, f], wbuf[f], dims, preferred_element_type=jnp.float32).T
+        got_im = lax.dot_general(fine[1, f], wbuf[f], dims, preferred_element_type=jnp.float32).T
         beam_re = got_re[:beams] - got_im[beams:]
         beam_im = got_re[beams:] + got_im[:beams]
         power = beam_re * beam_re + beam_im * beam_im
@@ -363,11 +385,15 @@
         table, incoming.reshape(2 * devices, per, samples), beams, delays, box_total
     )
     box_scores = box_scores.reshape(box_total, per, delays // 2).transpose(1, 0, 2)
-    step = 1
-    while step < blocks:
-        pairs = [(spot, spot ^ step) for spot in range(devices)]
-        peaks = jnp.maximum(peaks, lax.ppermute(peaks, "freq", pairs))
-        step *= 2
+    steps = [1 << bit for bit in range(1, blocks.bit_length() - 1)]
+    phases = [(a, b, a + b) for a, b in zip(steps[::2], steps[1::2])]
+    phases += [(step,) for step in steps[len(phases) * 2 :]] + [(1,)]
+    for phase in phases if blocks > 1 else []:
+        arrived = [
+            lax.ppermute(peaks, "freq", [(spot, spot ^ step) for spot in range(devices)]) for step in phase
+        ]
+        for piece in arrived:
+            peaks = jnp.maximum(peaks, piece)
     return (dedispersed, box_scores, peaks.reshape(beams))
 
 

time: 40.3 us -> 36.9 us (0.916)
  waiting for transfers between devices: 14.4 us -> 9.41 us
  starting transfers between devices: 8.05 us -> 11 us
  Pallas kernels: 13 us -> 11.7 us
    ppermute x3 -> x4, waiting for transfers between devices: 7.03 us -> 2 us  [shards(): lax.ppermute(peaks, 'freq', [(spot, spot ^ step) for spot in range(device...]
    ppermute x3 -> x4, starting transfers between devices: 0.62 us -> 3.56 us  [shards(): lax.ppermute(peaks, 'freq', [(spot, spot ^ step) for spot in range(device...]
    pallas_call x1, Pallas kernels: 7.99 us -> 6.75 us  [k1(): pl.pallas_call(functools.partial(k1_kernel, chunk), out_shape=jax.ShapeDt...]
  transfers between devices with their start and end apart: 4 -> 5, of which waited for: 4 -> 4; matrix products, arithmetic and copies ran while one was open for 8% -> 9% of each run, Pallas kernels for 0% -> 0%
where the time goes in v5:
time: 36.9 us; the launch traced here: 36.6 us
  Pallas kernels  11.7 us (32%)
  starting transfers between devices  11 us (30%)
  waiting for transfers between devices  9.41 us (26%)
  other arithmetic  3 us (8%)
  local copies, waits for them, and re-layouts  0.78 us (2%)
  between operations  0.7 us (2%)
    all_to_all x1, starting transfers between devices, shards(): lax.all_to_all(outgoing, 'freq', split_axis=0, concat_axis=0, tiled=True)  7.43 us
    all_to_all x1, waiting for transfers between devices, shards(): lax.all_to_all(outgoing, 'freq', split_axis=0, concat_axis=0, tiled=True)  7.41 us
    pallas_call x1, Pallas kernels, k1(): pl.pallas_call(functools.partial(k1_kernel, chunk), out_shape=jax.ShapeDt...  6.75 us
    pallas_call x1, Pallas kernels, k2(): pl.pallas_call(k2_kernel, out_shape=(jax.ShapeDtypeStruct((per, half_rows...  4.98 us
    ppermute x4, starting transfers between devices, shards(): lax.ppermute(peaks, 'freq', [(spot, spot ^ step) for spot in range(device...  3.56 us
    ppermute x4, waiting for transfers between devices, shards(): lax.ppermute(peaks, 'freq', [(spot, spot ^ step) for spot in range(device...  2 us
    mul x1, other arithmetic, merge_table(): part = jnp.stack([(base + low) * per, (base + child + high) * per, low])  0.82 us
    squeeze x1, other arithmetic, merge_table(): low, high = (offsets[level, 0], offsets[level, 1])  0.77 us
  transfers between devices with their start and end apart: 5, of which 4 were waited for; matrix products, arithmetic and copies ran while one was open for 9% of the time, Pallas kernels for 0%

profile of v5, /device:TPU:0, one launch (start us, length us, event | category | flops | bytes accessed | tf_op | source)
XLA Modules:
  0.0 36.6 jit_solution(13004029902867007816)
XLA Ops:
  0.6 6.7 %channelize.1 = f32[2,8,2,8,256]{4,3,2,1,0:T(8,128)} custom-call(f32[2,8]{1,0:T(2,128)} %bitcast.79, bf16[526,16,2,128]{3,2,1,0:T(2,128)(2,1)} %bitcast.75, bf16[2,128,2048]{2,1,0:T(8,128)(2,1)} %bitcast.77), custom_call_target="tpu_custom_call" | custom-call | tf_op jit(solution)/shard_map/channelize/pallas_call | solution.py:116
  7.4 7.4 %all-to-all-start = ((f32[16,2,8,256]{3,2,1,0:T(8,128)}), f32[16,2,8,256]{3,2,1,0:T(8,128)S(1)}, u32[]{:S(2)}, u32[]{:S(2)}) async-start(f32[16,2,8,256]{3,2,1,0:T(8,128)} %bitcast.76), calls=%async_computation | async-start | bytes 524288 | tf_op jit(solution)/shard_map/all_to_all | solution.py:381
  14.8 0.8 %slice_bitcast_fusion.6 = (s32[1,128]{1,0:T(1,128)S(1)}, s32[1,1,128]{2,1,0:T(1,128)S(1)}, s32[1,128]{1,0:T(1,128)S(1)}, s32[1,128]{1,0:T(1,128)S(1)}, s32[1,128...) fusion(s32[5,2,128]{2,1,0:T(2,128)} %param.8), kind=kLoop, calls=%fused_computation.45 | loop fusion | flops 768 | bytes 7168 | tf_op jit(solution)/shard_map/squeeze | solution.py:146
  15.6 0.8 %add_multiply_fusion = (s32[1,128]{1,0:T(1,128)S(1)}, s32[1,128]{1,0:T(1,128)S(1)}, s32[1,128]{1,0:T(1,128)S(1)}, s32[1,128]{1,0:T(1,128)S(1)}, s32[1,128]{1,0:T...) fusion(s32[5,2,128]{2,1,0:T(2,128)} %param.8), kind=kLoop, calls=%fused_computation.28 | loop fusion | flops 3840 | bytes 10240 | tf_op jit(solution)/shard_map/mul | solution.py:147
  16.4 0.1 slice_bitcast_fusion.1
  16.6 0.1 constant_dynamic-update-slice_fusion
  16.7 0.7 %pad_add_fusion.2 = s32[9]{0:T(128)S(1)} fusion(s32[1]{0:T(128)} %bitcast.16, s32[8]{0:T(128)} %param.9), kind=kLoop, calls=%fused_computation.15 | loop fusion | flops 9 | bytes 72 | tf_op jit(solution)/shard_map/concatenate | solution.py:153
  17.4 7.4 %all-to-all-done = f32[16,2,8,256]{3,2,1,0:T(8,128)S(1)} async-done(((f32[16,2,8,256]{3,2,1,0:T(8,128)}), f32[16,2,8,256]{3,2,1,0:T(8,128)S(1)}, u32[]{:S(2)}, u32[]{:S(2)}) %all-to-all-start) | async-done | bytes 262176 | tf_op jit(solution)/shard_map/all_to_all | solution.py:381
  24.8 5.0 %dedisperse.1 = (f32[8,64,256]{2,1,0:T(8,128)}, f32[8,512]{1,0:T(8,128)S(1)}, f32[1,64]{1,0:T(1,128)S(1)}) custom-call(s32[2048]{0:T(1024)S(1)} %pad_add_fusion.table_hbm, f32[32,8,256]{2,1,0:T(8,128)S(1)} %bitcast.74), custom_call_target="tpu_custom_call" | custom-call | tf_op jit(solution)/shard_map/dedisperse/pallas_call | solution.py:346
  29.8 0.6 %collective-permute-start.2 = (f32[1,64]{1,0:T(1,128)S(1)}, f32[1,64]{1,0:T(1,128)S(1)}, u32[]{:S(2)}, u32[]{:S(2)}) collective-permute-start(f32[1,64]{1,0:T(1,128)S(1)} %get-tuple-element.8), channel_id=1, source_target_pairs={{0,6},{1,7},{2,4},{3,5},{4,2},{5,3},{6,0},{7,1},{8,14},{9,15},{10,... | collective-permute-start | bytes 776 | tf_op jit(solution)/shard_map/ppermute | solution.py:393
  30.4 0.0 collective-permute-start.1
  30.4 3.0 %collective-permute-start = (f32[1,64]{1,0:T(1,128)S(1)}, f32[1,64]{1,0:T(1,128)S(1)}, u32[]{:S(2)}, u32[]{:S(2)}) collective-permute-start(f32[1,64]{1,0:T(1,128)S(1)} %get-tuple-element.8), channel_id=1, source_target_pairs={{0,2},{1,3},{2,0},{3,1},{4,6},{5,7},{6,4},{7,5},{8,10},{9,11},{10,... | collective-permute-start | bytes 776 | tf_op jit(solution)/shard_map/ppermute | solution.py:393
  33.4 1.0 %collective-permute-done.2 = f32[1,64]{1,0:T(1,128)S(1)} collective-permute-done((f32[1,64]{1,0:T(1,128)S(1)}, f32[1,64]{1,0:T(1,128)S(1)}, u32[]{:S(2)}, u32[]{:S(2)}) %collective-permute-start.2) | collective-permute-done | bytes 288 | tf_op jit(solution)/shard_map/ppermute | solution.py:393
  34.4 0.0 collective-permute-done.1
  34.4 0.6 %collective-permute-done = f32[1,64]{1,0:T(1,128)S(1)} collective-permute-done((f32[1,64]{1,0:T(1,128)S(1)}, f32[1,64]{1,0:T(1,128)S(1)}, u32[]{:S(2)}, u32[]{:S(2)}) %collective-permute-start) | collective-permute-done | bytes 288 | tf_op jit(solution)/shard_map/ppermute | solution.py:393
  34.9 0.0 collective-permute-start.3
  34.9 0.1 reshape.260
  35.0 0.6 %copy.10 = f32[8,8,64]{2,0,1:T(8,128)} copy(f32[8,8,64]{2,1,0:T(8,128)S(1)} %reshape.260) | data formatting | bytes 32768 | tf_op jit(solution)/shard_map/reshape | solution.py:387
  35.6 0.5 %collective-permute-done.3 = f32[1,64]{1,0:T(1,128)S(1)} collective-permute-done((f32[1,64]{1,0:T(1,128)S(1)}, f32[1,64]{1,0:T(1,128)S(1)}, u32[]{:S(2)}, u32[]{:S(2)}) %collective-permute-start.3) | collective-permute-done | bytes 288 | tf_op jit(solution)/shard_map/ppermute | solution.py:393
  36.1 0.5 %maximum_bitcast_fusion = f32[64]{0:T(128)} fusion(f32[1,64]{1,0:T(1,128)S(1)} %maximum_maximum_fusion, f32[1,64]{1,0:T(1,128)S(1)} %collective-permute-done.3), kind=kLoop, calls=%fused_computation.26 | loop fusion | flops 64 | bytes 768 | tf_op jit(solution)/shard_map/reshape | solution.py:397
  (8 shorter events, 0.1 us)
Async XLA Ops:
  7.4 17.4 %all-to-all-start = ((f32[16,2,8,256]{3,2,1,0:T(8,128)}), f32[16,2,8,256]{3,2,1,0:T(8,128)S(1)}, u32[]{:S(2)}, u32[]{:S(2)}) async-start(f32[16,2,8,256]{3,2,1,0:T(8,128)} %bitcast.76), calls=%async_computation | async-start | bytes 524288 | tf_op jit(solution)/shard_map/all_to_all | solution.py:381
  29.8 4.5 %collective-permute-start.2 = (f32[1,64]{1,0:T(1,128)S(1)}, f32[1,64]{1,0:T(1,128)S(1)}, u32[]{:S(2)}, u32[]{:S(2)}) collective-permute-start(f32[1,64]{1,0:T(1,128)S(1)} %get-tuple-element.8), channel_id=1, source_target_pairs={{0,6},{1,7},{2,4},{3,5},{4,2},{5,3},{6,0},{7,1},{8,14},{9,15},{10,... | collective-permute-start | bytes 776 | tf_op jit(solution)/shard_map/ppermute | solution.py:393
  30.4 4.0 %collective-permute-start.1 = (f32[1,64]{1,0:T(1,128)S(1)}, f32[1,64]{1,0:T(1,128)S(1)}, u32[]{:S(2)}, u32[]{:S(2)}) collective-permute-start(f32[1,64]{1,0:T(1,128)S(1)} %get-tuple-element.8), channel_id=1, source_target_pairs={{0,4},{1,5},{2,6},{3,7},{4,0},{5,1},{6,2},{7,3},{8,12},{9,13},{10,... | collective-permute-start | bytes 776 | tf_op jit(solution)/shard_map/ppermute | solution.py:393
  30.4 4.5 %collective-permute-start = (f32[1,64]{1,0:T(1,128)S(1)}, f32[1,64]{1,0:T(1,128)S(1)}, u32[]{:S(2)}, u32[]{:S(2)}) collective-permute-start(f32[1,64]{1,0:T(1,128)S(1)} %get-tuple-element.8), channel_id=1, source_target_pairs={{0,2},{1,3},{2,0},{3,1},{4,6},{5,7},{6,4},{7,5},{8,10},{9,11},{10,... | collective-permute-start | bytes 776 | tf_op jit(solution)/shard_map/ppermute | solution.py:393
  34.9 1.2 %collective-permute-start.3 = (f32[1,64]{1,0:T(1,128)S(1)}, f32[1,64]{1,0:T(1,128)S(1)}, u32[]{:S(2)}, u32[]{:S(2)}) collective-permute-start(f32[1,64]{1,0:T(1,128)S(1)} %maximum_maximum_fusion), channel_id=1, source_target_pairs={{0,1},{1,0},{2,3},{3,2},{4,5},{5,4},{6,7},{7,6},{8,9},{9,8},{10,11... | collective-permute-start | bytes 776 | tf_op jit(solution)/shard_map/ppermute | solution.py:393

commit v6 on v5

--- a/solution.py
+++ b/solution.py
@@ -8,8 +8,6 @@
 from jax.experimental.pallas import tpu as pltpu
 from jax.sharding import PartitionSpec as P
 
-
-PAIRS = 4
 
 def k1_kernel(chunk, taps_hbm, x_hbm, w_hbm, out_ref, slab, wbuf, fine, taps_ref, x_sem, w_sem, taps_sem):
     branches, tap_total = taps_ref.shape
@@ -57,14 +55,13 @@
         pieces = [flat[2 * g + i, pl.ds(4 * s0, reach), :] for i in range(2)]
         return jnp.concatenate(pieces, 1)
 
-    def pairs(h, carry):
+    def pairs(first, many):
         work = []
-        for u in range(PAIRS):
-            g = PAIRS * h + u
+        for u in range(many):
+            g = first + u
             work += [(g, *span) for span in spans]
-        for u in range(PAIRS):
-            x_copy(2 * (PAIRS * h + u)).wait()
-            x_copy(2 * (PAIRS * h + u) + 1).wait()
+        for u in range(2 * many):
+            x_copy(2 * first + u).wait()
         ahead = load(*work[0])
         for n, (g, s0, size, _) in enumerate(work):
             here = ahead
@@ -73,16 +70,19 @@
             got = jnp.dot(filters[size], here, preferred_element_type=jnp.float32)
             rounded = (got[: 4 * size] + got[4 * size :]).astype(jnp.bfloat16)
             for q in range(4):
-                fine[q // 2, q % 2, pl.ds(s0, size), pl.ds(pl.multiple_of(256 * g, 256), 256)] = rounded[
+                fine[q // 2, q % 2, pl.ds(s0, size), pl.ds(256 * g, 256)] = rounded[
                     q * size : (q + 1) * size
                 ]
-        return carry
 
     for j in range(tiles):
         spare = slab.shape[1] - rows_in
         if spare:
             slab[j, pl.ds(rows_in, spare)] = jnp.zeros((spare, 2, 128), jnp.bfloat16)
-    lax.fori_loop(0, tiles // 2 // PAIRS, pairs, 0)
+    place = 0
+    pair_total = tiles // 2
+    for many in (1, pair_total // 2 - 1, pair_total - pair_total // 2):
+        pairs(place, many)
+        place += many
     w_copy.wait()
     for f in range(2):
         dims = (((1,), (1,)), ((), ()))
@@ -133,7 +133,7 @@
 
 
 UNROLL = 128
-RAMPS = 4
+RAMPS = 8
 
 
 def merge_table(offsets, boxes, half, block, per):

time: 36.9 us -> 36.5 us (0.989)
  Pallas kernels: 11.7 us -> 11.3 us
where the time goes in v6:
time: 36.5 us; the launch traced here: 36.1 us
  Pallas kernels  11.3 us (31%)
  starting transfers between devices  11 us (30%)
  waiting for transfers between devices  9.41 us (26%)
  other arithmetic  3 us (8%)
  local copies, waits for them, and re-layouts  0.78 us (2%)
  between operations  0.7 us (2%)
    all_to_all x1, starting transfers between devices, shards(): lax.all_to_all(outgoing, 'freq', split_axis=0, concat_axis=0, tiled=True)  7.43 us
    all_to_all x1, waiting for transfers between devices, shards(): lax.all_to_all(outgoing, 'freq', split_axis=0, concat_axis=0, tiled=True)  7.41 us
    pallas_call x1, Pallas kernels, k1(): pl.pallas_call(functools.partial(k1_kernel, chunk), out_shape=jax.ShapeDt...  6.45 us
    pallas_call x1, Pallas kernels, k2(): pl.pallas_call(k2_kernel, out_shape=(jax.ShapeDtypeStruct((per, half_rows...  4.81 us
    ppermute x4, starting transfers between devices, shards(): lax.ppermute(peaks, 'freq', [(spot, spot ^ step) for spot in range(device...  3.56 us
    ppermute x4, waiting for transfers between devices, shards(): lax.ppermute(peaks, 'freq', [(spot, spot ^ step) for spot in range(device...  2 us
    mul x1, other arithmetic, merge_table(): part = jnp.stack([(base + low) * per, (base + child + high) * per, low])  0.82 us
    squeeze x1, other arithmetic, merge_table(): low, high = (offsets[level, 0], offsets[level, 1])  0.77 us
  transfers between devices with their start and end apart: 5, of which 4 were waited for; matrix products, arithmetic and copies ran while one was open for 9% of the time, Pallas kernels for 0%

profile of v6, /device:TPU:0, one launch (start us, length us, event | category | flops | bytes accessed | tf_op | source)
XLA Modules:
  0.0 36.1 jit_solution(17184182607724540194)
XLA Ops:
  0.6 6.5 %channelize.1 = f32[2,8,2,8,256]{4,3,2,1,0:T(8,128)} custom-call(f32[2,8]{1,0:T(2,128)} %bitcast.79, bf16[526,16,2,128]{3,2,1,0:T(2,128)(2,1)} %bitcast.75, bf16[2,128,2048]{2,1,0:T(8,128)(2,1)} %bitcast.77), custom_call_target="tpu_custom_call" | custom-call | tf_op jit(solution)/shard_map/channelize/pallas_call | solution.py:116
  7.1 7.4 %all-to-all-start = ((f32[16,2,8,256]{3,2,1,0:T(8,128)}), f32[16,2,8,256]{3,2,1,0:T(8,128)S(1)}, u32[]{:S(2)}, u32[]{:S(2)}) async-start(f32[16,2,8,256]{3,2,1,0:T(8,128)} %bitcast.76), calls=%async_computation | async-start | bytes 524288 | tf_op jit(solution)/shard_map/all_to_all | solution.py:381
  14.5 0.8 %slice_bitcast_fusion.6 = (s32[1,128]{1,0:T(1,128)S(1)}, s32[1,1,128]{2,1,0:T(1,128)S(1)}, s32[1,128]{1,0:T(1,128)S(1)}, s32[1,128]{1,0:T(1,128)S(1)}, s32[1,128...) fusion(s32[5,2,128]{2,1,0:T(2,128)} %param.8), kind=kLoop, calls=%fused_computation.45 | loop fusion | flops 768 | bytes 7168 | tf_op jit(solution)/shard_map/squeeze | solution.py:146
  15.3 0.8 %add_multiply_fusion = (s32[1,128]{1,0:T(1,128)S(1)}, s32[1,128]{1,0:T(1,128)S(1)}, s32[1,128]{1,0:T(1,128)S(1)}, s32[1,128]{1,0:T(1,128)S(1)}, s32[1,128]{1,0:T...) fusion(s32[5,2,128]{2,1,0:T(2,128)} %param.8), kind=kLoop, calls=%fused_computation.28 | loop fusion | flops 3840 | bytes 10240 | tf_op jit(solution)/shard_map/mul | solution.py:147
  16.1 0.1 slice_bitcast_fusion.1
  16.3 0.1 constant_dynamic-update-slice_fusion
  16.4 0.7 %pad_add_fusion.2 = s32[9]{0:T(128)S(1)} fusion(s32[1]{0:T(128)} %bitcast.16, s32[8]{0:T(128)} %param.9), kind=kLoop, calls=%fused_computation.15 | loop fusion | flops 9 | bytes 72 | tf_op jit(solution)/shard_map/concatenate | solution.py:153
  17.1 7.4 %all-to-all-done = f32[16,2,8,256]{3,2,1,0:T(8,128)S(1)} async-done(((f32[16,2,8,256]{3,2,1,0:T(8,128)}), f32[16,2,8,256]{3,2,1,0:T(8,128)S(1)}, u32[]{:S(2)}, u32[]{:S(2)}) %all-to-all-start) | async-done | bytes 262176 | tf_op jit(solution)/shard_map/all_to_all | solution.py:381
  24.5 4.8 %dedisperse.1 = (f32[8,64,256]{2,1,0:T(8,128)}, f32[8,512]{1,0:T(8,128)S(1)}, f32[1,64]{1,0:T(1,128)S(1)}) custom-call(s32[2048]{0:T(1024)S(1)} %pad_add_fusion.table_hbm, f32[32,8,256]{2,1,0:T(8,128)S(1)} %bitcast.74), custom_call_target="tpu_custom_call" | custom-call | tf_op jit(solution)/shard_map/dedisperse/pallas_call | solution.py:346
  29.3 0.6 %collective-permute-start.2 = (f32[1,64]{1,0:T(1,128)S(1)}, f32[1,64]{1,0:T(1,128)S(1)}, u32[]{:S(2)}, u32[]{:S(2)}) collective-permute-start(f32[1,64]{1,0:T(1,128)S(1)} %get-tuple-element.8), channel_id=1, source_target_pairs={{0,6},{1,7},{2,4},{3,5},{4,2},{5,3},{6,0},{7,1},{8,14},{9,15},{10,... | collective-permute-start | bytes 776 | tf_op jit(solution)/shard_map/ppermute | solution.py:393
  29.9 0.0 collective-permute-start.1
  29.9 3.0 %collective-permute-start = (f32[1,64]{1,0:T(1,128)S(1)}, f32[1,64]{1,0:T(1,128)S(1)}, u32[]{:S(2)}, u32[]{:S(2)}) collective-permute-start(f32[1,64]{1,0:T(1,128)S(1)} %get-tuple-element.8), channel_id=1, source_target_pairs={{0,2},{1,3},{2,0},{3,1},{4,6},{5,7},{6,4},{7,5},{8,10},{9,11},{10,... | collective-permute-start | bytes 776 | tf_op jit(solution)/shard_map/ppermute | solution.py:393
  32.9 1.0 %collective-permute-done.2 = f32[1,64]{1,0:T(1,128)S(1)} collective-permute-done((f32[1,64]{1,0:T(1,128)S(1)}, f32[1,64]{1,0:T(1,128)S(1)}, u32[]{:S(2)}, u32[]{:S(2)}) %collective-permute-start.2) | collective-permute-done | bytes 288 | tf_op jit(solution)/shard_map/ppermute | solution.py:393
  33.9 0.0 collective-permute-done.1
  33.9 0.6 %collective-permute-done = f32[1,64]{1,0:T(1,128)S(1)} collective-permute-done((f32[1,64]{1,0:T(1,128)S(1)}, f32[1,64]{1,0:T(1,128)S(1)}, u32[]{:S(2)}, u32[]{:S(2)}) %collective-permute-start) | collective-permute-done | bytes 288 | tf_op jit(solution)/shard_map/ppermute | solution.py:393
  34.5 0.0 collective-permute-start.3
  34.5 0.1 reshape.260
  34.5 0.6 %copy.10 = f32[8,8,64]{2,0,1:T(8,128)} copy(f32[8,8,64]{2,1,0:T(8,128)S(1)} %reshape.260) | data formatting | bytes 32768 | tf_op jit(solution)/shard_map/reshape | solution.py:387
  35.2 0.5 %collective-permute-done.3 = f32[1,64]{1,0:T(1,128)S(1)} collective-permute-done((f32[1,64]{1,0:T(1,128)S(1)}, f32[1,64]{1,0:T(1,128)S(1)}, u32[]{:S(2)}, u32[]{:S(2)}) %collective-permute-start.3) | collective-permute-done | bytes 288 | tf_op jit(solution)/shard_map/ppermute | solution.py:393
  35.6 0.5 %maximum_bitcast_fusion = f32[64]{0:T(128)} fusion(f32[1,64]{1,0:T(1,128)S(1)} %maximum_maximum_fusion, f32[1,64]{1,0:T(1,128)S(1)} %collective-permute-done.3), kind=kLoop, calls=%fused_computation.26 | loop fusion | flops 64 | bytes 768 | tf_op jit(solution)/shard_map/reshape | solution.py:397
  (8 shorter events, 0.1 us)
Async XLA Ops:
  7.1 17.4 %all-to-all-start = ((f32[16,2,8,256]{3,2,1,0:T(8,128)}), f32[16,2,8,256]{3,2,1,0:T(8,128)S(1)}, u32[]{:S(2)}, u32[]{:S(2)}) async-start(f32[16,2,8,256]{3,2,1,0:T(8,128)} %bitcast.76), calls=%async_computation | async-start | bytes 524288 | tf_op jit(solution)/shard_map/all_to_all | solution.py:381
  29.3 4.5 %collective-permute-start.2 = (f32[1,64]{1,0:T(1,128)S(1)}, f32[1,64]{1,0:T(1,128)S(1)}, u32[]{:S(2)}, u32[]{:S(2)}) collective-permute-start(f32[1,64]{1,0:T(1,128)S(1)} %get-tuple-element.8), channel_id=1, source_target_pairs={{0,6},{1,7},{2,4},{3,5},{4,2},{5,3},{6,0},{7,1},{8,14},{9,15},{10,... | collective-permute-start | bytes 776 | tf_op jit(solution)/shard_map/ppermute | solution.py:393
  29.9 4.0 %collective-permute-start.1 = (f32[1,64]{1,0:T(1,128)S(1)}, f32[1,64]{1,0:T(1,128)S(1)}, u32[]{:S(2)}, u32[]{:S(2)}) collective-permute-start(f32[1,64]{1,0:T(1,128)S(1)} %get-tuple-element.8), channel_id=1, source_target_pairs={{0,4},{1,5},{2,6},{3,7},{4,0},{5,1},{6,2},{7,3},{8,12},{9,13},{10,... | collective-permute-start | bytes 776 | tf_op jit(solution)/shard_map/ppermute | solution.py:393
  29.9 4.5 %collective-permute-start = (f32[1,64]{1,0:T(1,128)S(1)}, f32[1,64]{1,0:T(1,128)S(1)}, u32[]{:S(2)}, u32[]{:S(2)}) collective-permute-start(f32[1,64]{1,0:T(1,128)S(1)} %get-tuple-element.8), channel_id=1, source_target_pairs={{0,2},{1,3},{2,0},{3,1},{4,6},{5,7},{6,4},{7,5},{8,10},{9,11},{10,... | collective-permute-start | bytes 776 | tf_op jit(solution)/shard_map/ppermute | solution.py:393
  34.5 1.2 %collective-permute-start.3 = (f32[1,64]{1,0:T(1,128)S(1)}, f32[1,64]{1,0:T(1,128)S(1)}, u32[]{:S(2)}, u32[]{:S(2)}) collective-permute-start(f32[1,64]{1,0:T(1,128)S(1)} %maximum_maximum_fusion), channel_id=1, source_target_pairs={{0,1},{1,0},{2,3},{3,2},{4,5},{5,4},{6,7},{7,6},{8,9},{9,8},{10,11... | collective-permute-start | bytes 776 | tf_op jit(solution)/shard_map/ppermute | solution.py:393

commit v7 on v6

--- a/solution.py
+++ b/solution.py
@@ -9,7 +9,7 @@
 from jax.sharding import PartitionSpec as P
 
 
-def k1_kernel(chunk, taps_hbm, x_hbm, w_hbm, out_ref, slab, wbuf, fine, taps_ref, x_sem, w_sem, taps_sem):
+def k1_kernel(chunk, taps_hbm, x_hbm, w_hbm, out_ref, slab, wbuf, fine, ready, taps_ref, x_sem, w_sem, taps_sem, out_sem):
     branches, tap_total = taps_ref.shape
     rows_in, tiles = x_hbm.shape[0], x_hbm.shape[1]
     samples = fine.shape[2]
@@ -84,6 +84,11 @@
         pairs(place, many)
         place += many
     w_copy.wait()
+    sends = []
+
+    def spots(f):
+        return [out_ref.at[h, :, f] for h in range(2)] if len(out_ref.shape) == 5 else [out_ref.at[f]]
+
     for f in range(2):
         dims = (((1,), (1,)), ((), ()))
         got_re = lax.dot_general(fine[0, f], wbuf[f], dims, preferred_element_type=jnp.float32).T
@@ -95,12 +100,13 @@
         centered = power - level
         spread = jnp.mean(centered * centered, axis=-1, keepdims=True)
         normed = centered / jnp.sqrt(spread + 1e-05)
-        if out_ref.ndim == 5:
-            normed = normed.reshape(out_ref.shape[1], out_ref.shape[3], samples)
-            for h in range(2):
-                out_ref[h, :, f] = normed
-        else:
-            out_ref[f] = normed
+        ready[f] = normed.reshape(ready.shape[1:])
+        sends += [pltpu.make_async_copy(ready.at[f], spot, out_sem.at[len(sends) + n]) for n, spot in enumerate(spots(f))]
+        for send in sends[-len(spots(f)) :]:
+            send.start()
+    for send in sends:
+        send.wait()
+
 
 def k1(taps, volume, steering, per):
     t, branches, parts, antennas = volume.shape
@@ -117,15 +123,17 @@
         functools.partial(k1_kernel, chunk),
         out_shape=jax.ShapeDtypeStruct(out_dims, jnp.float32),
         in_specs=[pl.BlockSpec(memory_space=pltpu.HBM)] * 3,
-        out_specs=pl.BlockSpec(memory_space=pltpu.VMEM),
+        out_specs=pl.BlockSpec(memory_space=pl.ANY),
         scratch_shapes=[
             pltpu.VMEM((tiles, depth // 2, 2, 128), jnp.bfloat16),
             pltpu.VMEM((2, 2 * beams, antennas), jnp.bfloat16),
             pltpu.VMEM((2, 2, samples, antennas), jnp.bfloat16),
+            pltpu.VMEM((2,) + ((beams // per, per) if per % 8 == 0 else (beams,)) + (samples,), jnp.float32),
             pltpu.SMEM((2, tap_total), jnp.float32),
             pltpu.SemaphoreType.DMA((tiles,)),
             pltpu.SemaphoreType.DMA,
             pltpu.SemaphoreType.DMA,
+            pltpu.SemaphoreType.DMA((4,)),
         ],
         compiler_params=pltpu.CompilerParams(vmem_limit_bytes=67043328),
         name="channelize",

time: 36.5 us -> 36.5 us (level)
  no operation moved by 1% of the time
where the time goes in v7:
time: 36.5 us; the launch traced here: 36.1 us
  Pallas kernels  11.3 us (31%)
  starting transfers between devices  11 us (30%)
  waiting for transfers between devices  9.41 us (26%)
  other arithmetic  3 us (8%)
  local copies, waits for them, and re-layouts  0.78 us (2%)
  between operations  0.7 us (2%)
    all_to_all x1, starting transfers between devices, shards(): lax.all_to_all(outgoing, 'freq', split_axis=0, concat_axis=0, tiled=True)  7.43 us
    all_to_all x1, waiting for transfers between devices, shards(): lax.all_to_all(outgoing, 'freq', split_axis=0, concat_axis=0, tiled=True)  7.41 us
    pallas_call x1, Pallas kernels, k1(): pl.pallas_call(functools.partial(k1_kernel, chunk), out_shape=jax.ShapeDt...  6.43 us
    pallas_call x1, Pallas kernels, k2(): pl.pallas_call(k2_kernel, out_shape=(jax.ShapeDtypeStruct((per, half_rows...  4.83 us
    ppermute x4, starting transfers between devices, shards(): lax.ppermute(peaks, 'freq', [(spot, spot ^ step) for spot in range(device...  3.56 us
    ppermute x4, waiting for transfers between devices, shards(): lax.ppermute(peaks, 'freq', [(spot, spot ^ step) for spot in range(device...  2 us
    mul x1, other arithmetic, merge_table(): part = jnp.stack([(base + low) * per, (base + child + high) * per, low])  0.82 us
    squeeze x1, other arithmetic, merge_table(): low, high = (offsets[level, 0], offsets[level, 1])  0.77 us
  transfers between devices with their start and end apart: 5, of which 4 were waited for; matrix products, arithmetic and copies ran while one was open for 9% of the time, Pallas kernels for 0%

profile of v7, /device:TPU:0, one launch (start us, length us, event | category | flops | bytes accessed | tf_op | source)
XLA Modules:
  0.0 36.1 jit_solution(9183649287560209488)
XLA Ops:
  0.6 6.4 %channelize.1 = f32[2,8,2,8,256]{4,3,2,1,0:T(8,128)} custom-call(f32[2,8]{1,0:T(2,128)} %bitcast.79, bf16[526,16,2,128]{3,2,1,0:T(2,128)(2,1)} %bitcast.75, bf16[2,128,2048]{2,1,0:T(8,128)(2,1)} %bitcast.77), custom_call_target="tpu_custom_call" | custom-call | tf_op jit(solution)/shard_map/channelize/pallas_call | solution.py:122
  7.1 7.4 %all-to-all-start = ((f32[16,2,8,256]{3,2,1,0:T(8,128)}), f32[16,2,8,256]{3,2,1,0:T(8,128)S(1)}, u32[]{:S(2)}, u32[]{:S(2)}) async-start(f32[16,2,8,256]{3,2,1,0:T(8,128)} %bitcast.76), calls=%async_computation | async-start | bytes 524288 | tf_op jit(solution)/shard_map/all_to_all | solution.py:389
  14.5 0.8 %slice_bitcast_fusion.6 = (s32[1,128]{1,0:T(1,128)S(1)}, s32[1,1,128]{2,1,0:T(1,128)S(1)}, s32[1,128]{1,0:T(1,128)S(1)}, s32[1,128]{1,0:T(1,128)S(1)}, s32[1,128...) fusion(s32[5,2,128]{2,1,0:T(2,128)} %param.8), kind=kLoop, calls=%fused_computation.45 | loop fusion | flops 768 | bytes 7168 | tf_op jit(solution)/shard_map/squeeze | solution.py:154
  15.3 0.8 %add_multiply_fusion = (s32[1,128]{1,0:T(1,128)S(1)}, s32[1,128]{1,0:T(1,128)S(1)}, s32[1,128]{1,0:T(1,128)S(1)}, s32[1,128]{1,0:T(1,128)S(1)}, s32[1,128]{1,0:T...) fusion(s32[5,2,128]{2,1,0:T(2,128)} %param.8), kind=kLoop, calls=%fused_computation.28 | loop fusion | flops 3840 | bytes 10240 | tf_op jit(solution)/shard_map/mul | solution.py:155
  16.1 0.1 slice_bitcast_fusion.1
  16.3 0.1 constant_dynamic-update-slice_fusion
  16.4 0.7 %pad_add_fusion.2 = s32[9]{0:T(128)S(1)} fusion(s32[1]{0:T(128)} %bitcast.16, s32[8]{0:T(128)} %param.9), kind=kLoop, calls=%fused_computation.15 | loop fusion | flops 9 | bytes 72 | tf_op jit(solution)/shard_map/concatenate | solution.py:161
  17.1 7.4 %all-to-all-done = f32[16,2,8,256]{3,2,1,0:T(8,128)S(1)} async-done(((f32[16,2,8,256]{3,2,1,0:T(8,128)}), f32[16,2,8,256]{3,2,1,0:T(8,128)S(1)}, u32[]{:S(2)}, u32[]{:S(2)}) %all-to-all-start) | async-done | bytes 262176 | tf_op jit(solution)/shard_map/all_to_all | solution.py:389
  24.5 4.8 %dedisperse.1 = (f32[8,64,256]{2,1,0:T(8,128)}, f32[8,512]{1,0:T(8,128)S(1)}, f32[1,64]{1,0:T(1,128)S(1)}) custom-call(s32[2048]{0:T(1024)S(1)} %pad_add_fusion.table_hbm, f32[32,8,256]{2,1,0:T(8,128)S(1)} %bitcast.74), custom_call_target="tpu_custom_call" | custom-call | tf_op jit(solution)/shard_map/dedisperse/pallas_call | solution.py:354
  29.4 0.6 %collective-permute-start.2 = (f32[1,64]{1,0:T(1,128)S(1)}, f32[1,64]{1,0:T(1,128)S(1)}, u32[]{:S(2)}, u32[]{:S(2)}) collective-permute-start(f32[1,64]{1,0:T(1,128)S(1)} %get-tuple-element.8), channel_id=1, source_target_pairs={{0,6},{1,7},{2,4},{3,5},{4,2},{5,3},{6,0},{7,1},{8,14},{9,15},{10,... | collective-permute-start | bytes 776 | tf_op jit(solution)/shard_map/ppermute | solution.py:401
  29.9 0.0 collective-permute-start.1
  29.9 3.0 %collective-permute-start = (f32[1,64]{1,0:T(1,128)S(1)}, f32[1,64]{1,0:T(1,128)S(1)}, u32[]{:S(2)}, u32[]{:S(2)}) collective-permute-start(f32[1,64]{1,0:T(1,128)S(1)} %get-tuple-element.8), channel_id=1, source_target_pairs={{0,2},{1,3},{2,0},{3,1},{4,6},{5,7},{6,4},{7,5},{8,10},{9,11},{10,... | collective-permute-start | bytes 776 | tf_op jit(solution)/shard_map/ppermute | solution.py:401
  32.9 1.0 %collective-permute-done.2 = f32[1,64]{1,0:T(1,128)S(1)} collective-permute-done((f32[1,64]{1,0:T(1,128)S(1)}, f32[1,64]{1,0:T(1,128)S(1)}, u32[]{:S(2)}, u32[]{:S(2)}) %collective-permute-start.2) | collective-permute-done | bytes 288 | tf_op jit(solution)/shard_map/ppermute | solution.py:401
  33.9 0.0 collective-permute-done.1
  33.9 0.6 %collective-permute-done = f32[1,64]{1,0:T(1,128)S(1)} collective-permute-done((f32[1,64]{1,0:T(1,128)S(1)}, f32[1,64]{1,0:T(1,128)S(1)}, u32[]{:S(2)}, u32[]{:S(2)}) %collective-permute-start) | collective-permute-done | bytes 288 | tf_op jit(solution)/shard_map/ppermute | solution.py:401
  34.5 0.0 collective-permute-start.3
  34.5 0.1 reshape.260
  34.5 0.6 %copy.10 = f32[8,8,64]{2,0,1:T(8,128)} copy(f32[8,8,64]{2,1,0:T(8,128)S(1)} %reshape.260) | data formatting | bytes 32768 | tf_op jit(solution)/shard_map/reshape | solution.py:395
  35.2 0.5 %collective-permute-done.3 = f32[1,64]{1,0:T(1,128)S(1)} collective-permute-done((f32[1,64]{1,0:T(1,128)S(1)}, f32[1,64]{1,0:T(1,128)S(1)}, u32[]{:S(2)}, u32[]{:S(2)}) %collective-permute-start.3) | collective-permute-done | bytes 288 | tf_op jit(solution)/shard_map/ppermute | solution.py:401
  35.6 0.5 %maximum_bitcast_fusion = f32[64]{0:T(128)} fusion(f32[1,64]{1,0:T(1,128)S(1)} %maximum_maximum_fusion, f32[1,64]{1,0:T(1,128)S(1)} %collective-permute-done.3), kind=kLoop, calls=%fused_computation.26 | loop fusion | flops 64 | bytes 768 | tf_op jit(solution)/shard_map/reshape | solution.py:405
  (8 shorter events, 0.1 us)
Async XLA Ops:
  7.1 17.4 %all-to-all-start = ((f32[16,2,8,256]{3,2,1,0:T(8,128)}), f32[16,2,8,256]{3,2,1,0:T(8,128)S(1)}, u32[]{:S(2)}, u32[]{:S(2)}) async-start(f32[16,2,8,256]{3,2,1,0:T(8,128)} %bitcast.76), calls=%async_computation | async-start | bytes 524288 | tf_op jit(solution)/shard_map/all_to_all | solution.py:389
  29.4 4.5 %collective-permute-start.2 = (f32[1,64]{1,0:T(1,128)S(1)}, f32[1,64]{1,0:T(1,128)S(1)}, u32[]{:S(2)}, u32[]{:S(2)}) collective-permute-start(f32[1,64]{1,0:T(1,128)S(1)} %get-tuple-element.8), channel_id=1, source_target_pairs={{0,6},{1,7},{2,4},{3,5},{4,2},{5,3},{6,0},{7,1},{8,14},{9,15},{10,... | collective-permute-start | bytes 776 | tf_op jit(solution)/shard_map/ppermute | solution.py:401
  29.9 4.0 %collective-permute-start.1 = (f32[1,64]{1,0:T(1,128)S(1)}, f32[1,64]{1,0:T(1,128)S(1)}, u32[]{:S(2)}, u32[]{:S(2)}) collective-permute-start(f32[1,64]{1,0:T(1,128)S(1)} %get-tuple-element.8), channel_id=1, source_target_pairs={{0,4},{1,5},{2,6},{3,7},{4,0},{5,1},{6,2},{7,3},{8,12},{9,13},{10,... | collective-permute-start | bytes 776 | tf_op jit(solution)/shard_map/ppermute | solution.py:401
  29.9 4.5 %collective-permute-start = (f32[1,64]{1,0:T(1,128)S(1)}, f32[1,64]{1,0:T(1,128)S(1)}, u32[]{:S(2)}, u32[]{:S(2)}) collective-permute-start(f32[1,64]{1,0:T(1,128)S(1)} %get-tuple-element.8), channel_id=1, source_target_pairs={{0,2},{1,3},{2,0},{3,1},{4,6},{5,7},{6,4},{7,5},{8,10},{9,11},{10,... | collective-permute-start | bytes 776 | tf_op jit(solution)/shard_map/ppermute | solution.py:401
  34.5 1.2 %collective-permute-start.3 = (f32[1,64]{1,0:T(1,128)S(1)}, f32[1,64]{1,0:T(1,128)S(1)}, u32[]{:S(2)}, u32[]{:S(2)}) collective-permute-start(f32[1,64]{1,0:T(1,128)S(1)} %maximum_maximum_fusion), channel_id=1, source_target_pairs={{0,1},{1,0},{2,3},{3,2},{4,5},{5,4},{6,7},{7,6},{8,9},{9,8},{10,11... | collective-permute-start | bytes 776 | tf_op jit(solution)/shard_map/ppermute | solution.py:401

commit v8 on v6

--- a/solution.py
+++ b/solution.py
@@ -208,7 +208,7 @@
         total = total + normed_ref[c]
     common = total * (1.0 / channels)
 
-    group = min(4, channels)
+    group = min(8, channels)
 
     def put(level, t, row, value):
         rows = pl.ds(row * per if isinstance(row, int) else pl.multiple_of(row * per, per), per)

time: 36.5 us -> 36.3 us (level)
  no operation moved by 1% of the time
where the time goes in v8:
time: 36.3 us; the launch traced here: 36 us
  Pallas kernels  11.1 us (31%)
  starting transfers between devices  11 us (30%)
  waiting for transfers between devices  9.41 us (26%)
  other arithmetic  3 us (8%)
  local copies, waits for them, and re-layouts  0.78 us (2%)
  between operations  0.7 us (2%)
    all_to_all x1, starting transfers between devices, shards(): lax.all_to_all(outgoing, 'freq', split_axis=0, concat_axis=0, tiled=True)  7.43 us
    all_to_all x1, waiting for transfers between devices, shards(): lax.all_to_all(outgoing, 'freq', split_axis=0, concat_axis=0, tiled=True)  7.41 us
    pallas_call x1, Pallas kernels, k1(): pl.pallas_call(functools.partial(k1_kernel, chunk), out_shape=jax.ShapeDt...  6.45 us
    pallas_call x1, Pallas kernels, k2(): pl.pallas_call(k2_kernel, out_shape=(jax.ShapeDtypeStruct((per, half_rows...  4.64 us
    ppermute x4, starting transfers between devices, shards(): lax.ppermute(peaks, 'freq', [(spot, spot ^ step) for spot in range(device...  3.56 us
    ppermute x4, waiting for transfers between devices, shards(): lax.ppermute(peaks, 'freq', [(spot, spot ^ step) for spot in range(device...  2 us
    mul x1, other arithmetic, merge_table(): part = jnp.stack([(base + low) * per, (base + child + high) * per, low])  0.82 us
    squeeze x1, other arithmetic, merge_table(): low, high = (offsets[level, 0], offsets[level, 1])  0.77 us
  transfers between devices with their start and end apart: 5, of which 4 were waited for; matrix products, arithmetic and copies ran while one was open for 9% of the time, Pallas kernels for 0%

profile of v8, /device:TPU:0, one launch (start us, length us, event | category | flops | bytes accessed | tf_op | source)
XLA Modules:
  0.0 36.0 jit_solution(4281278168049219845)
XLA Ops:
  0.6 6.5 %channelize.1 = f32[2,8,2,8,256]{4,3,2,1,0:T(8,128)} custom-call(f32[2,8]{1,0:T(2,128)} %bitcast.79, bf16[526,16,2,128]{3,2,1,0:T(2,128)(2,1)} %bitcast.75, bf16[2,128,2048]{2,1,0:T(8,128)(2,1)} %bitcast.77), custom_call_target="tpu_custom_call" | custom-call | tf_op jit(solution)/shard_map/channelize/pallas_call | solution.py:116
  7.1 7.4 %all-to-all-start = ((f32[16,2,8,256]{3,2,1,0:T(8,128)}), f32[16,2,8,256]{3,2,1,0:T(8,128)S(1)}, u32[]{:S(2)}, u32[]{:S(2)}) async-start(f32[16,2,8,256]{3,2,1,0:T(8,128)} %bitcast.76), calls=%async_computation | async-start | bytes 524288 | tf_op jit(solution)/shard_map/all_to_all | solution.py:381
  14.5 0.8 %slice_bitcast_fusion.6 = (s32[1,128]{1,0:T(1,128)S(1)}, s32[1,1,128]{2,1,0:T(1,128)S(1)}, s32[1,128]{1,0:T(1,128)S(1)}, s32[1,128]{1,0:T(1,128)S(1)}, s32[1,128...) fusion(s32[5,2,128]{2,1,0:T(2,128)} %param.8), kind=kLoop, calls=%fused_computation.45 | loop fusion | flops 768 | bytes 7168 | tf_op jit(solution)/shard_map/squeeze | solution.py:146
  15.3 0.8 %add_multiply_fusion = (s32[1,128]{1,0:T(1,128)S(1)}, s32[1,128]{1,0:T(1,128)S(1)}, s32[1,128]{1,0:T(1,128)S(1)}, s32[1,128]{1,0:T(1,128)S(1)}, s32[1,128]{1,0:T...) fusion(s32[5,2,128]{2,1,0:T(2,128)} %param.8), kind=kLoop, calls=%fused_computation.28 | loop fusion | flops 3840 | bytes 10240 | tf_op jit(solution)/shard_map/mul | solution.py:147
  16.1 0.1 slice_bitcast_fusion.1
  16.3 0.1 constant_dynamic-update-slice_fusion
  16.4 0.7 %pad_add_fusion.2 = s32[9]{0:T(128)S(1)} fusion(s32[1]{0:T(128)} %bitcast.16, s32[8]{0:T(128)} %param.9), kind=kLoop, calls=%fused_computation.15 | loop fusion | flops 9 | bytes 72 | tf_op jit(solution)/shard_map/concatenate | solution.py:153
  17.1 7.4 %all-to-all-done = f32[16,2,8,256]{3,2,1,0:T(8,128)S(1)} async-done(((f32[16,2,8,256]{3,2,1,0:T(8,128)}), f32[16,2,8,256]{3,2,1,0:T(8,128)S(1)}, u32[]{:S(2)}, u32[]{:S(2)}) %all-to-all-start) | async-done | bytes 262176 | tf_op jit(solution)/shard_map/all_to_all | solution.py:381
  24.5 4.6 %dedisperse.1 = (f32[8,64,256]{2,1,0:T(8,128)}, f32[8,512]{1,0:T(8,128)S(1)}, f32[1,64]{1,0:T(1,128)S(1)}) custom-call(s32[2048]{0:T(1024)S(1)} %pad_add_fusion.table_hbm, f32[32,8,256]{2,1,0:T(8,128)S(1)} %bitcast.74), custom_call_target="tpu_custom_call" | custom-call | tf_op jit(solution)/shard_map/dedisperse/pallas_call | solution.py:346
  29.2 0.6 %collective-permute-start.2 = (f32[1,64]{1,0:T(1,128)S(1)}, f32[1,64]{1,0:T(1,128)S(1)}, u32[]{:S(2)}, u32[]{:S(2)}) collective-permute-start(f32[1,64]{1,0:T(1,128)S(1)} %get-tuple-element.8), channel_id=1, source_target_pairs={{0,6},{1,7},{2,4},{3,5},{4,2},{5,3},{6,0},{7,1},{8,14},{9,15},{10,... | collective-permute-start | bytes 776 | tf_op jit(solution)/shard_map/ppermute | solution.py:393
  29.7 0.0 collective-permute-start.1
  29.7 3.0 %collective-permute-start = (f32[1,64]{1,0:T(1,128)S(1)}, f32[1,64]{1,0:T(1,128)S(1)}, u32[]{:S(2)}, u32[]{:S(2)}) collective-permute-start(f32[1,64]{1,0:T(1,128)S(1)} %get-tuple-element.8), channel_id=1, source_target_pairs={{0,2},{1,3},{2,0},{3,1},{4,6},{5,7},{6,4},{7,5},{8,10},{9,11},{10,... | collective-permute-start | bytes 776 | tf_op jit(solution)/shard_map/ppermute | solution.py:393
  32.7 1.0 %collective-permute-done.2 = f32[1,64]{1,0:T(1,128)S(1)} collective-permute-done((f32[1,64]{1,0:T(1,128)S(1)}, f32[1,64]{1,0:T(1,128)S(1)}, u32[]{:S(2)}, u32[]{:S(2)}) %collective-permute-start.2) | collective-permute-done | bytes 288 | tf_op jit(solution)/shard_map/ppermute | solution.py:393
  33.7 0.0 collective-permute-done.1
  33.7 0.6 %collective-permute-done = f32[1,64]{1,0:T(1,128)S(1)} collective-permute-done((f32[1,64]{1,0:T(1,128)S(1)}, f32[1,64]{1,0:T(1,128)S(1)}, u32[]{:S(2)}, u32[]{:S(2)}) %collective-permute-start) | collective-permute-done | bytes 288 | tf_op jit(solution)/shard_map/ppermute | solution.py:393
  34.3 0.0 collective-permute-start.3
  34.3 0.1 reshape.260
  34.4 0.6 %copy.10 = f32[8,8,64]{2,0,1:T(8,128)} copy(f32[8,8,64]{2,1,0:T(8,128)S(1)} %reshape.260) | data formatting | bytes 32768 | tf_op jit(solution)/shard_map/reshape | solution.py:387
  35.0 0.5 %collective-permute-done.3 = f32[1,64]{1,0:T(1,128)S(1)} collective-permute-done((f32[1,64]{1,0:T(1,128)S(1)}, f32[1,64]{1,0:T(1,128)S(1)}, u32[]{:S(2)}, u32[]{:S(2)}) %collective-permute-start.3) | collective-permute-done | bytes 288 | tf_op jit(solution)/shard_map/ppermute | solution.py:393
  35.5 0.5 %maximum_bitcast_fusion = f32[64]{0:T(128)} fusion(f32[1,64]{1,0:T(1,128)S(1)} %maximum_maximum_fusion, f32[1,64]{1,0:T(1,128)S(1)} %collective-permute-done.3), kind=kLoop, calls=%fused_computation.26 | loop fusion | flops 64 | bytes 768 | tf_op jit(solution)/shard_map/reshape | solution.py:397
  (8 shorter events, 0.1 us)
Async XLA Ops:
  7.1 17.4 %all-to-all-start = ((f32[16,2,8,256]{3,2,1,0:T(8,128)}), f32[16,2,8,256]{3,2,1,0:T(8,128)S(1)}, u32[]{:S(2)}, u32[]{:S(2)}) async-start(f32[16,2,8,256]{3,2,1,0:T(8,128)} %bitcast.76), calls=%async_computation | async-start | bytes 524288 | tf_op jit(solution)/shard_map/all_to_all | solution.py:381
  29.2 4.5 %collective-permute-start.2 = (f32[1,64]{1,0:T(1,128)S(1)}, f32[1,64]{1,0:T(1,128)S(1)}, u32[]{:S(2)}, u32[]{:S(2)}) collective-permute-start(f32[1,64]{1,0:T(1,128)S(1)} %get-tuple-element.8), channel_id=1, source_target_pairs={{0,6},{1,7},{2,4},{3,5},{4,2},{5,3},{6,0},{7,1},{8,14},{9,15},{10,... | collective-permute-start | bytes 776 | tf_op jit(solution)/shard_map/ppermute | solution.py:393
  29.7 4.0 %collective-permute-start.1 = (f32[1,64]{1,0:T(1,128)S(1)}, f32[1,64]{1,0:T(1,128)S(1)}, u32[]{:S(2)}, u32[]{:S(2)}) collective-permute-start(f32[1,64]{1,0:T(1,128)S(1)} %get-tuple-element.8), channel_id=1, source_target_pairs={{0,4},{1,5},{2,6},{3,7},{4,0},{5,1},{6,2},{7,3},{8,12},{9,13},{10,... | collective-permute-start | bytes 776 | tf_op jit(solution)/shard_map/ppermute | solution.py:393
  29.7 4.5 %collective-permute-start = (f32[1,64]{1,0:T(1,128)S(1)}, f32[1,64]{1,0:T(1,128)S(1)}, u32[]{:S(2)}, u32[]{:S(2)}) collective-permute-start(f32[1,64]{1,0:T(1,128)S(1)} %get-tuple-element.8), channel_id=1, source_target_pairs={{0,2},{1,3},{2,0},{3,1},{4,6},{5,7},{6,4},{7,5},{8,10},{9,11},{10,... | collective-permute-start | bytes 776 | tf_op jit(solution)/shard_map/ppermute | solution.py:393
  34.3 1.2 %collective-permute-start.3 = (f32[1,64]{1,0:T(1,128)S(1)}, f32[1,64]{1,0:T(1,128)S(1)}, u32[]{:S(2)}, u32[]{:S(2)}) collective-permute-start(f32[1,64]{1,0:T(1,128)S(1)} %maximum_maximum_fusion), channel_id=1, source_target_pairs={{0,1},{1,0},{2,3},{3,2},{4,5},{5,4},{6,7},{7,6},{8,9},{9,8},{10,11... | collective-permute-start | bytes 776 | tf_op jit(solution)/shard_map/ppermute | solution.py:393
